TPU v7x, 128 devices: a whole 4x4x4 slice. The times are simulated.
128 devices in a mesh: node: 8 (over y, core), outer: 16 (over z, x).
Axes of the slice: x: 4, y: 4, z: 4, core: 2. Of those that a mesh axis runs over, the one named last changes fastest.
Arguments:
- embeddings: bfloat16 [393216, 1024], P(('node', 'outer')), may hold values from -6 to 6
- embedding_parent_index: int32 [393216], P(('node', 'outer')), may hold values from 0 to 511, as said below
- parent_slot: int32 [512], replicated, may hold values from 0 to 511, each once
- centroids: bfloat16 [128, 512, 1024], P(None, 'outer'), may hold values from -6 to 6
Outputs:
- new_children: float32 [128, 512, 1024], P('node', 'outer')
- new_parents: float32 [512, 1024], P('outer')
Inputs may be any that keep to these rules, and one draw needn't show every extreme that they name: `embedding_parent_index`: within each device's 3072 rows the ids never fall; every parent has at least 3 and at most 12 rows on every device, and some parent has exactly 12 rows on every device. `parent_slot`: each slot once; slot s lies on index s // 32 of outer.
All inputs are finite; a program needn't handle non-finite values.
Results may differ from a plain program's by a relative error of at most 0.0029.
Values may be sent and summed in bfloat16 or wider, within the bound.
No kernel may reach another device: no remote copies, remote signals or barrier semaphores. Data moves between devices by JAX's collectives and lax.ppermute only.
A program may use at most 192 MiB of HBM per device.

v0:
```python
import jax
import jax.numpy as jnp
from jax import lax
from jax.sharding import PartitionSpec as P

softness_level = 0.1
prior_weight = 0.25


def unit_scale(values):
    return values * lax.rsqrt(jnp.mean(values * values, axis=-1, keepdims=True) + 1e-06)


def pack_rows(
    unit_rows, embedding_parent_index, parent_slot, wanted_slots, capacity, parents_block
):
    row_total, feature_count = unit_rows.shape
    parent_total = parent_slot.shape[0]
    parent_range = jnp.arange(parent_total, dtype=jnp.int32)
    parent_counts = jnp.sum(
        (embedding_parent_index[None, :] == parent_range[:, None]).astype(jnp.int32), axis=1
    )
    parent_first = jnp.sum(
        (embedding_parent_index[None, :] < parent_range[:, None]).astype(jnp.int32), axis=1
    )
    window_rows = parents_block * capacity
    padded_rows = jnp.concatenate(
        [unit_rows, jnp.zeros((window_rows, feature_count), unit_rows.dtype)], axis=0
    )
    window_range = jnp.arange(window_rows, dtype=jnp.int32)
    slot_place = window_range % capacity

    def one_block(unused_carry, block_number):
        base_parent = block_number * parents_block
        block_first = lax.dynamic_slice_in_dim(parent_first, base_parent, parents_block)
        block_counts = lax.dynamic_slice_in_dim(parent_counts, base_parent, parents_block)
        window_start = block_first[0]
        window_piece = lax.dynamic_slice_in_dim(padded_rows, window_start, window_rows, 0)
        target_row = jnp.repeat(block_first, capacity) + slot_place - window_start
        is_live = slot_place < jnp.repeat(block_counts, capacity)
        selector = ((target_row[:, None] == window_range[None, :]) & is_live[:, None]).astype(
            jnp.bfloat16
        )
        picked = jnp.dot(selector, window_piece, preferred_element_type=jnp.float32).astype(
            jnp.bfloat16
        )
        return (unused_carry, picked)

    block_numbers = jnp.arange(parent_total // parents_block, dtype=jnp.int32)
    _, block_rows_all = lax.scan(one_block, jnp.zeros((), jnp.int32), block_numbers)
    in_order = block_rows_all.reshape(parent_total, capacity * feature_count)
    mover = (parent_slot[None, :] == wanted_slots[:, None]).astype(jnp.bfloat16)
    reordered = jnp.dot(mover, in_order, preferred_element_type=jnp.float32).astype(jnp.bfloat16)
    return reordered.reshape(wanted_slots.shape[0], capacity, feature_count)


def soft_weights(arrived, low_children, shrink_multiplier):
    logits = (
        jnp.einsum("pmd,kpd->pmk", arrived, low_children, preferred_element_type=jnp.float32)
        * shrink_multiplier
    )
    return jax.nn.softmax(logits, axis=-1).astype(jnp.bfloat16)


def body(embeddings, embedding_parent_index, parent_slot, centroids):
    rows_here, embedding_feature = embeddings.shape
    children_count, owned_slots, _ = centroids.shape
    parent_count = parent_slot.shape[0]
    capacity = 2 * ((rows_here + parent_count - 1) // parent_count)
    shrink_multiplier = 1.0 / (softness_level * embedding_feature)
    nodes = lax.axis_size("node")
    outers = lax.axis_size("outer")
    node_index = lax.axis_index("node")
    unit_rows = unit_scale(embeddings.astype(jnp.float32)).astype(jnp.bfloat16)
    unit_children = unit_scale(centroids.astype(jnp.float32))
    low_children = unit_children.astype(jnp.bfloat16)
    all_slots = jnp.arange(parent_count, dtype=jnp.int32)
    packed = pack_rows(
        unit_rows, embedding_parent_index, parent_slot, all_slots, capacity, owned_slots
    )
    packed = packed.reshape(outers, owned_slots, capacity, embedding_feature)
    arrived = lax.all_to_all(packed, "outer", split_axis=0, concat_axis=2, tiled=True)[0]
    weights = soft_weights(arrived, low_children, shrink_multiplier)
    per_node = children_count // nodes
    child_total = lax.psum_scatter(
        jnp.einsum("pmk,pmd->kpd", weights, arrived, preferred_element_type=jnp.float32),
        "node",
        scatter_dimension=0,
        tiled=True,
    )
    own_children = lax.dynamic_slice_in_dim(unit_children, node_index * per_node, per_node, 0)
    new_children = unit_scale(prior_weight * own_children + child_total)
    coarse_total = lax.psum(jnp.sum(new_children, axis=0), "node")
    new_parents = unit_scale(coarse_total)
    return (new_children, new_parents)


def solution(mesh):
    placed = (P(("node", "outer"), None), P(("node", "outer")), P(), P(None, "outer", None))
    return jax.shard_map(
        body,
        mesh=mesh,
        in_specs=placed,
        out_specs=(P("node", "outer", None), P("outer", None)),
        check_vma=False,
    )
```

profile of v0, /device:TPU:1, one launch (start us, length us, event | category | flops | bytes accessed | tf_op | source)
XLA Modules:
  0.0 607.2 jit_solution(3324919384820335201)
XLA Ops:
  7.2 2.3 convert_reduce_fusion
  9.5 4.1 fusion.20
  13.6 3.7 fusion.21
  17.3 6.4 %concatenate.3 = bf16[3456,1024]{1,0:T(8,128)(2,1)} pad(bf16[3072,1024]{1,0:T(8,128)(2,1)} %fusion.21, bf16[]{:T(256)} %constant.23.clone.1), padding=0_384x0_0 | pad | bytes 13369346 | tf_op jit(solution)/shard_map/concatenate | solution.py:27
  23.7 74.2 %while.12 = (s32[]{:T(128)}, bf16[16,384,1024]{2,1,0:T(8,128)(2,1)}, s32[16]{0:T(128)S(1)}, s32[512]{0:T(512)S(1)}, s32[512]{0:T(512)S(1)}, /*index=5*/bf16[3456...) while((s32[]{:T(128)}, ...), condition=%wide.region_5.6_spmd.clone.clone, body=%wide.region_4.5_spmd.clone.clone.sunk | while | flops 302683776 | bytes 1590489 | solution.py:50
  23.9 0.6 dynamic_slice.38
  25.8 2.7 fusion.57
  28.5 0.6 dynamic_slice.38
  30.4 2.7 fusion.57
  33.1 0.6 dynamic_slice.38
  35.0 2.7 fusion.57
  37.7 0.6 dynamic_slice.38
  39.7 2.7 fusion.57
  42.3 0.6 dynamic_slice.38
  44.3 2.7 fusion.57
  46.9 0.6 dynamic_slice.38
  48.9 2.7 fusion.57
  51.5 0.6 dynamic_slice.38
  53.5 2.7 fusion.57
  56.2 0.6 dynamic_slice.38
  58.1 2.7 fusion.57
  62.8 2.7 fusion.57
  65.4 0.6 dynamic_slice.38
  67.4 2.7 fusion.57
  72.0 2.7 fusion.57
  76.6 2.8 fusion.57
  81.3 2.7 fusion.57
  85.9 2.7 fusion.57
  90.6 2.7 fusion.57
  95.2 2.7 fusion.57
  97.9 24.4 %reshape.68 = bf16[512,12288]{1,0:T(8,128)(2,1)} reshape(bf16[16,384,1024]{2,1,0:T(8,128)(2,1)} %get-tuple-element.47) | data formatting | bytes 25165824 | tf_op jit(solution)/shard_map/reshape | solution.py:51
  122.3 14.1 %convolution_convert_fusion.1 = bf16[512,12288]{1,0:T(8,128)(2,1)} fusion(bf16[512,12288]{1,0:T(8,128)(2,1)} %reshape.68, s32[512]{0:T(512)S(1)} %copy-done.1), kind=kOutput, calls=%fused_computation.22 | convolution fusion | flops 6449004544 | bytes 25167872 | tf_op jit(solution)/shard_map/dot_general | solution.py:53
  136.4 20.7 %reshape_reshape.3 = bf16[16,32,12,1024]{3,2,1,0:T(8,128)(2,1)} reshape(bf16[512,12288]{1,0:T(8,128)(2,1)} %convolution_convert_fusion.1) | data formatting | bytes 25165824 | tf_op jit(solution)/shard_map/reshape;reshape | solution.py:81
  157.1 13.1 %copy.21 = bf16[16,32,12,1024]{3,1,2,0:T(8,128)(2,1)} copy(bf16[16,32,12,1024]{3,2,1,0:T(8,128)(2,1)} %reshape_reshape.3) | data formatting | bytes 25165824 | tf_op jit(solution)/shard_map/reshape;reshape | solution.py:81
  170.2 8.5 %all-to-all-start = ((bf16[16,32,12,1024]{3,1,2,0:T(8,128)(2,1)}), bf16[16,32,12,1024]{3,1,2,0:T(8,128)(2,1)}, u32[]{:S(2)}, u32[]{:S(2)}) async-start(bf16[16,32,12,1024]{3,1,2,0:T(8,128)(2,1)} %copy.21), calls=%async_computation | async-start | bytes 25165824 | tf_op jit(solution)/shard_map/all_to_all | solution.py:82
  178.7 5.1 fusion.19
  183.8 11.6 %convert_multiply_fusion = (f32[128,32,1024]{2,1,0:T(8,128)}, bf16[128,32,1024]{2,1,0:T(8,128)(2,1)}) fusion(bf16[128,32,1024]{2,1,0:T(8,128)(2,1)} %param.9, f32[128,32]{1,0:T(8,128)S(1)} %add_rsqrt_fusion), kind=kLoop, calls=%fused_computation.20 | loop fusion | flops 12582912 | bytes 33570816 | tf_op jit(solution)/shard_map/mul | solution.py:11
  195.5 169.4 %all-to-all-done = bf16[16,32,12,1024]{3,1,2,0:T(8,128)(2,1)} async-done(((bf16[16,32,12,1024]{3,1,2,0:T(8,128)(2,1)}), bf16[16,32,12,1024]{3,1,2,0:T(8,128)(2,1)}, u32[]{:S(2)}, u32[]{:S(2)}) %all-to-all-start) | async-done | bytes 12582944 | tf_op jit(solution)/shard_map/all_to_all | solution.py:82
  364.9 21.5 %fusion.22 = f32[32,192,128]{2,1,0:T(8,128)S(1)} fusion(bf16[32,192,1024]{2,0,1:T(8,128)(2,1)} %bitcast.2, bf16[128,32,1024]{2,1,0:T(8,128)(2,1)} %get-tuple-element.104), kind=kOutput, calls=%fused_computation.28 | convolution fusion | flops 1610612736 | bytes 24117248 | tf_op jit(solution)/shard_map/pmd,kpd->pmk/dot_general | solution.py:59
  386.4 2.0 fusion.46
  388.4 35.6 %fusion.26 = f32[128,32,1024]{0,2,1:T(8,128)} fusion(bf16[32,192,1024]{2,0,1:T(8,128)(2,1)} %bitcast.2, f32[32,192]{1,0:T(8,128)S(1)} %fusion.46, f32[32,192,128]{2,1,0:T(8,128)S(1)} %fusion.22), kind=kOutput, calls=%fused_computation.32 | convolution fusion | flops 1614551168 | bytes 32530432 | tf_op jit(solution)/shard_map/pmk,pmd->kpd/dot_general | solution.py:86
  424.0 16.6 %copy.25 = f32[128,32,1024]{2,1,0:T(8,128)} copy(f32[128,32,1024]{0,2,1:T(8,128)} %fusion.26) | data formatting | bytes 33554432 | tf_op jit(solution)/shard_map/pmk,pmd->kpd/transpose | solution.py:86
  440.7 91.4 %reduce-scatter.2.cloned.1.call-done = f32[16,32,1024]{2,1,0:T(8,128)} async-done(((f32[128,32,1024]{2,1,0:T(8,128)}), f32[16,32,1024]{2,1,0:T(8,128)}) %reduce-scatter.2.cloned.1.call-update) | async-done | bytes 2097168 | tf_op jit(solution)/shard_map/reduce_scatter | solution.py:85
  532.0 2.6 multiply_reduce_fusion.1
  534.6 4.5 fusion.45
  539.2 58.1 %all-reduce.3.cloned.1.call-done = f32[32,1024]{1,0:T(8,128)} async-done(((f32[32,1024]{1,0:T(8,128)}), f32[32,1024]{1,0:T(8,128)}) %all-reduce.3.cloned.1.call-update) | async-done | bytes 131088 | tf_op jit(solution)/shard_map/psum | solution.py:93
  597.3 1.0 multiply_reduce_fusion.2
  598.3 1.6 broadcast_multiply_fusion.1
  (149 shorter events, 13.5 us)
Async XLA Ops:
  7.2 6.4 %copy-start = (bf16[3072,1024]{1,0:T(8,128)(2,1)S(1)}, bf16[3072,1024]{1,0:T(8,128)(2,1)}, u32[]{:S(2)}) copy-start(bf16[3072,1024]{1,0:T(8,128)(2,1)} %param.6) | copy-start | bytes 18874372
  97.9 24.4 %copy-start.1 = (s32[512]{0:T(512)S(1)}, s32[512]{0:T(512)}, u32[]{:S(2)}) copy-start(s32[512]{0:T(512)} %param.8) | copy-start | bytes 6148
  170.2 194.7 %all-to-all-start = ((bf16[16,32,12,1024]{3,1,2,0:T(8,128)(2,1)}), bf16[16,32,12,1024]{3,1,2,0:T(8,128)(2,1)}, u32[]{:S(2)}, u32[]{:S(2)}) async-start(bf16[16,32,12,1024]{3,1,2,0:T(8,128)(2,1)} %copy.21), calls=%async_computation | async-start | bytes 25165824 | tf_op jit(solution)/shard_map/all_to_all | solution.py:82
  178.7 353.4 %reduce-scatter.2.cloned.1.call-start = ((), (), s32[]{:S(2)}) async-start(), calls=%async_computation.2 | async-start | bytes 18874368 | tf_op jit(solution)/shard_map/reduce_scatter | solution.py:85
  440.6 156.7 %all-reduce.3.cloned.1.call-start = ((), (), s32[]{:S(2)}) async-start(), calls=%async_computation.3 | async-start | bytes 262144 | tf_op jit(solution)/shard_map/psum | solution.py:93
Sparse Core Ops, SparseCore 0:
  440.7 91.2 reduce-scatter.1
  539.3 57.9 all-reduce.2
where the time goes:
time: 615 us; the launch traced here: 607 us
  waiting for transfers between devices  319 us (52%)
  matrix products  114 us (19%)
  local copies, waits for them, and re-layouts  98.6 us (16%)
  other arithmetic  39.7 us (6%)
  between operations  14.6 us (2%)
  loops' own time  12.6 us (2%)
  starting transfers between devices  8.54 us (1%)
    all_to_all x1, waiting for transfers between devices, body(): lax.all_to_all(packed, 'outer', split_axis=0, concat_axis=2, tiled=True)[0]  169 us
    reduce_scatter x1, waiting for transfers between devices, body(): lax.psum_scatter(jnp.einsum('pmk,pmd->kpd', weights, arrived, preferred_e...  91.4 us
    psum x1, waiting for transfers between devices, body(): coarse_total = lax.psum(jnp.sum(new_children, axis=0), 'node')  58.1 us
    dot_general x16, matrix products, one_block(): jnp.dot(selector, window_piece, preferred_element_type=jnp.float32)  43 us
    dot_general x1, matrix products, body(): jnp.einsum('pmk,pmd->kpd', weights, arrived, preferred_element_type=jnp.f...  35.6 us
    another operation x2, local copies, waits for them, and re-layouts, body(): packed = packed.reshape(outers, owned_slots, capacity, embedding_feature)  33.8 us
    reshape x1, local copies, waits for them, and re-layouts, pack_rows(): in_order = block_rows_all.reshape(parent_total, capacity * feature_count)  24.4 us
    dot_general x1, matrix products, soft_weights(): jnp.einsum('pmd,kpd->pmk', arrived, low_children, preferred_element_type=...  21.5 us
  transfers between devices with their start and end apart: 3, of which 3 were waited for; matrix products, arithmetic and copies ran while one was open for 3% of the time, Pallas kernels for 0%

commit v1 on v0

v1 whole, which is shorter than its diff:
```python
import functools

import jax
import jax.numpy as jnp
from jax import lax
from jax.experimental import pallas as pl
from jax.experimental.pallas import tpu as pltpu
from jax.sharding import PartitionSpec as P

softness_level = 0.1
prior_weight = 0.25
EPS = 1e-06

CAP = 12
OWN = 4
ROWS = OWN * CAP
TILE = 16
GROUPS = ROWS // TILE
PAIRS = 4
WIN = 32


def unit_scale(values):
    return values * lax.rsqrt(jnp.mean(values * values, axis=-1, keepdims=True) + EPS)


def pack_kernel(outers, owned, start_ref, count_ref, rows_ref, out_ref, unit_ref):
    total, width = rows_ref.shape
    step = pl.program_id(0)
    chunk = 64

    @pl.when(step == 0)
    def _():
        unit_ref[total:, :] = jnp.zeros((unit_ref.shape[0] - total, width), jnp.bfloat16)

        def normalise(i, carry):
            at = pl.ds(pl.multiple_of(i * chunk, chunk), chunk)
            unit_ref[at, :] = unit_scale(rows_ref[at, :].astype(jnp.float32)).astype(jnp.bfloat16)
            return carry

        lax.fori_loop(0, total // chunk, normalise, 0, unroll=4)

    row = lax.broadcasted_iota(jnp.int32, (2 * ROWS, 1), 0)
    half = (row >= ROWS).astype(jnp.int32)
    inner = row - half * ROWS
    group = lax.shift_right_logical(inner, 4)
    place = inner & (TILE - 1)
    first = place < CAP
    source = half * OWN + jnp.where(first, group, OWN - 1)
    position = jnp.where(first, place, group * (TILE - CAP) + place - CAP)
    column = lax.broadcasted_iota(jnp.int32, (2 * ROWS, 2 * OWN * WIN), 1)
    for pair in range(PAIRS):
        target = jnp.full((2 * ROWS, 1), -1, jnp.int32)
        windows = []
        for q in range(2 * OWN):
            device = (step * PAIRS + pair) * 2 + q // OWN
            slot = lax.rem(device, outers) * owned + lax.div(device, outers) * OWN + q % OWN
            start = start_ref[slot]
            count = count_ref[slot]
            aligned = lax.shift_left(lax.shift_right_logical(start, 4), 4)
            windows.append(unit_ref[pl.ds(pl.multiple_of(aligned, TILE), WIN), :])
            spot = q * WIN + (start - aligned) + position
            target = jnp.where((source == q) & (position < count), spot, target)
        selector = (column == target).astype(jnp.float32).astype(jnp.bfloat16)
        window = jnp.concatenate(windows, axis=0)
        out_ref[pair * 2 * ROWS : (pair + 1) * 2 * ROWS, :] = jnp.dot(
            selector, window, preferred_element_type=jnp.float32
        ).astype(jnp.bfloat16)


def pack(embeddings, starts, counts, outers, owned, devices):
    total, width = embeddings.shape
    return pl.pallas_call(
        functools.partial(pack_kernel, outers, owned),
        out_shape=jax.ShapeDtypeStruct((devices * ROWS, width), jnp.bfloat16),
        grid_spec=pltpu.PrefetchScalarGridSpec(
            num_scalar_prefetch=2,
            grid=(devices // (2 * PAIRS),),
            in_specs=[
                pl.BlockSpec((total, width), lambda i, s, c: (0, 0), pipeline_mode=pl.Buffered(1))
            ],
            out_specs=pl.BlockSpec((2 * ROWS * PAIRS, width), lambda i, s, c: (i, 0)),
            scratch_shapes=[pltpu.VMEM((total + WIN, width), jnp.bfloat16)],
        ),
        compiler_params=pltpu.CompilerParams(vmem_limit_bytes=40 << 20),
        name="pack",
    )(starts, counts, embeddings)


def sums_kernel(shrink, per_node, rows_ref, low_ref, unit_ref, out_ref, total_ref):
    step = pl.program_id(0)
    block, width = rows_ref.shape
    sources = block // ROWS
    children = low_ref.shape[1]

    @pl.when(step == 0)
    def _():
        total_ref[...] = jnp.zeros_like(total_ref)

    lane = lax.broadcasted_iota(jnp.int32, (1, sources * TILE), 1)
    first = (lane & (TILE - 1)) < CAP
    for g in range(GROUPS):
        rows = jnp.concatenate(
            [rows_ref[b * ROWS + g * TILE : b * ROWS + (g + 1) * TILE, :] for b in range(sources)],
            axis=0,
        )
        low = jnp.concatenate([low_ref[g], low_ref[OWN - 1]], axis=0)
        logits = lax.dot_general(
            low, rows, (((1,), (1,)), ((), ())), preferred_element_type=jnp.float32
        )
        chosen = jnp.where(first, logits[:children], logits[children:]) * shrink
        raised = jnp.exp(chosen)
        weights = raised / jnp.sum(raised, axis=0, keepdims=True)
        zero = jnp.zeros_like(weights)
        paired = jnp.concatenate(
            [jnp.where(first, weights, zero), jnp.where(first, zero, weights)], axis=0
        ).astype(jnp.bfloat16)
        sums = jnp.dot(paired, rows, preferred_element_type=jnp.float32)
        total_ref[g] += sums[:children]
        total_ref[OWN - 1] += sums[children:]

    @pl.when(step == pl.num_programs(0) - 1)
    def _():
        parents = []
        for j in range(OWN):
            fresh = unit_scale(prior_weight * unit_ref[j] + total_ref[j])
            parents.append(unit_scale(jnp.sum(fresh, axis=0, keepdims=True)))
            fresh = fresh.astype(jnp.bfloat16)
            for m in range(children // per_node):
                out_ref[m, j * per_node : (j + 1) * per_node, :] = fresh[
                    m * per_node : (m + 1) * per_node
                ]
        tail = jnp.concatenate(parents + parents, axis=0).astype(jnp.bfloat16)
        for m in range(children // per_node):
            out_ref[m, OWN * per_node :, :] = tail


def child_sums(arrived, low, unit, shrink, nodes):
    total, width = arrived.shape
    children = low.shape[1]
    per_node = children // nodes
    block = 32 * ROWS
    whole = lambda i: (0, 0, 0)
    return pl.pallas_call(
        functools.partial(sums_kernel, shrink, per_node),
        out_shape=jax.ShapeDtypeStruct((nodes, OWN * per_node + 2 * OWN, width), jnp.bfloat16),
        grid=(total // block,),
        in_specs=[
            pl.BlockSpec((block, width), lambda i: (i, 0)),
            pl.BlockSpec(low.shape, whole, pipeline_mode=pl.Buffered(1)),
            pl.BlockSpec(unit.shape, whole, pipeline_mode=pl.Buffered(1)),
        ],
        out_specs=pl.BlockSpec((nodes, OWN * per_node + 2 * OWN, width), whole),
        scratch_shapes=[pltpu.VMEM((OWN, children, width), jnp.float32)],
        compiler_params=pltpu.CompilerParams(vmem_limit_bytes=48 << 20),
        name="child_sums",
    )(arrived, low, unit)


def order_kernel(per_node, rows_ref, children_ref, parents_ref):
    block = OWN * per_node + 2 * OWN
    nodes = rows_ref.shape[0] // block
    slots = nodes * OWN
    column = lax.broadcasted_iota(jnp.int32, (1, rows_ref.shape[0]), 1)
    out = lax.broadcasted_iota(jnp.int32, (per_node * slots, 1), 0)
    slot = out & (slots - 1)
    child = lax.div(out, slots)
    wanted = lax.div(slot, OWN) * block + (slot & (OWN - 1)) * per_node + child
    mover = (wanted == column).astype(jnp.float32).astype(jnp.bfloat16)
    rows = rows_ref[...]
    children_ref[...] = jnp.dot(mover, rows, preferred_element_type=jnp.float32)
    slot = lax.broadcasted_iota(jnp.int32, (slots, 1), 0)
    wanted = lax.div(slot, OWN) * block + OWN * per_node + (slot & (OWN - 1))
    mover = (wanted == column).astype(jnp.float32).astype(jnp.bfloat16)
    parents_ref[...] = jnp.dot(mover, rows, preferred_element_type=jnp.float32)


def put_in_order(received, per_node):
    nodes, block, width = received.shape
    slots = nodes * OWN
    children, parents = pl.pallas_call(
        functools.partial(order_kernel, per_node),
        out_shape=(
            jax.ShapeDtypeStruct((per_node * slots, width), jnp.float32),
            jax.ShapeDtypeStruct((slots, width), jnp.float32),
        ),
        name="put_in_order",
    )(received.reshape(nodes * block, width))
    return children.reshape(per_node, slots, width), parents


def body(embeddings, embedding_parent_index, parent_slot, centroids):
    width = embeddings.shape[1]
    children, owned, _ = centroids.shape
    parent_count = parent_slot.shape[0]
    nodes = lax.axis_size("node")
    outers = lax.axis_size("outer")
    devices = nodes * outers
    shrink = 1.0 / (softness_level * width)
    node = lax.axis_index("node")

    ids = jnp.arange(parent_count, dtype=jnp.int32)
    held = (parent_slot[None, :] == ids[:, None]).astype(jnp.int32)
    parent_of_slot = jnp.sum(held * ids[None, :], axis=1)
    starts = jnp.sum(
        (embedding_parent_index[None, :] < parent_of_slot[:, None]).astype(jnp.int32), axis=1
    )
    counts = jnp.sum(
        (embedding_parent_index[None, :] == parent_of_slot[:, None]).astype(jnp.int32), axis=1
    )
    own = lax.dynamic_slice_in_dim(centroids, node * OWN, OWN, 1).transpose(1, 0, 2)
    unit = unit_scale(own.astype(jnp.float32))
    low = unit.astype(jnp.bfloat16)
    packed = pack(embeddings, starts, counts, outers, owned, devices)
    packed, unit, low = lax.optimization_barrier((packed, unit, low))
    arrived = lax.all_to_all(
        packed.reshape(devices, ROWS, width),
        ("node", "outer"),
        split_axis=0,
        concat_axis=0,
        tiled=True,
    )
    fresh = child_sums(
        arrived.reshape(devices * ROWS, width), low, unit, shrink, nodes
    )
    received = lax.all_to_all(fresh, "node", split_axis=0, concat_axis=0, tiled=True)
    return put_in_order(received, children // nodes)


def solution(mesh):
    placed = (P(("node", "outer"), None), P(("node", "outer")), P(), P(None, "outer", None))
    return jax.shard_map(
        body,
        mesh=mesh,
        in_specs=placed,
        out_specs=(P("node", "outer", None), P("outer", None)),
        check_vma=False,
    )
```

time: 615 us -> 211 us (0.34); the launches traced: 607 us -> 211 us
  waiting for transfers between devices: 319 us -> 0 us
  blocking collectives: 0 us -> 174 us
  matrix products: 114 us -> 0 us
  local copies, waits for them, and re-layouts: 98.6 us -> 2.6 us
  other arithmetic: 39.7 us -> 3.16 us
  Pallas kernels: 0 us -> 30.8 us
  between operations: 14.6 us -> 0.68 us
  loops' own time: 12.6 us -> 0 us
  starting transfers between devices: 8.54 us -> 0 us
    all_to_all x0 -> x2, blocking collectives: none -> 174 us  [the longest x1 153 us: body(): lax.all_to_all(packed.reshape(devices, ROWS, width), ('node', 'outer'), s...]
    all_to_all x1 -> x0, waiting for transfers between devices: 169 us -> none  [body(): lax.all_to_all(packed, 'outer', split_axis=0, concat_axis=2, tiled=True)[0]]
    dot_general x19 -> x0, matrix products: 114 us -> none  [the longest x16 43 us: one_block(): jnp.dot(selector, window_piece, preferred_element_type=jnp.float32)]
    reduce_scatter x1 -> x0, waiting for transfers between devices: 91.4 us -> none  [body(): lax.psum_scatter(jnp.einsum('pmk,pmd->kpd', weights, arrived, preferred_e...]
    psum x1 -> x0, waiting for transfers between devices: 58.1 us -> none  [body(): coarse_total = lax.psum(jnp.sum(new_children, axis=0), 'node')]
    another operation x2 -> x0, local copies, waits for them, and re-layouts: 33.8 us -> none  [body(): packed = packed.reshape(outers, owned_slots, capacity, embedding_feature)]
    pallas_call x0 -> x3, Pallas kernels: none -> 30.8 us  [the longest x1 15.1 us: pack(): pl.pallas_call(functools.partial(pack_kernel, outers, owned), out_shape=j...]
    reshape x33 -> x0, local copies, waits for them, and re-layouts: 27.8 us -> none  [the longest x1 24.4 us: pack_rows(): in_order = block_rows_all.reshape(parent_total, capacity * feature_count)]
  transfers between devices with their start and end apart: 3 -> 0, of which waited for: 3 -> 0; matrix products, arithmetic and copies ran while one was open for 3% -> 0% of each run, Pallas kernels for 0% -> 0%
where the time goes in v1:
time: 211 us
  blocking collectives  174 us (82%)
  Pallas kernels  30.8 us (15%)
  other arithmetic  3.16 us (1%)
  local copies, waits for them, and re-layouts  2.6 us (1%)
    all_to_all x1, blocking collectives, body(): lax.all_to_all(packed.reshape(devices, ROWS, width), ('node', 'outer'), s...  153 us
    all_to_all x1, blocking collectives, body(): lax.all_to_all(fresh, 'node', split_axis=0, concat_axis=0, tiled=True)  20.5 us
    pallas_call x1, Pallas kernels, pack(): pl.pallas_call(functools.partial(pack_kernel, outers, owned), out_shape=j...  15.1 us
    pallas_call x1, Pallas kernels, child_sums(): pl.pallas_call(functools.partial(sums_kernel, shrink, per_node), out_shap...  12.1 us

profile of v1, /device:TPU:1, one launch (start us, length us, event | category | flops | bytes accessed | tf_op | source)
XLA Modules:
  0.0 210.7 jit_solution(15877200695625000988)
XLA Ops:
  0.6 0.9 select_reduce_fusion
  1.5 0.0 copy-start
  1.5 2.3 %constant_dynamic-slice_fusion = bf16[128,4,1024]{2,1,0:T(4,128)(2,1)S(1)} fusion(bf16[128,32,1024]{2,1,0:T(8,128)(2,1)} %param.7, s32[]{:T(128)S(6)} %select_n.3), kind=kLoop, calls=%fused_computation.9 | loop fusion | bytes 2097156 | tf_op jit(solution)/shard_map/dynamic_slice | solution.py:211
  3.8 0.4 fusion
  4.2 0.0 copy-start.1
  4.2 0.4 fusion.1
  4.6 0.3 copy-done.1
  4.9 1.5 convert_reduce_fusion
  6.4 0.0 copy-done
  6.4 15.1 %pack.1 = bf16[6144,1024]{1,0:T(8,128)(2,1)} custom-call(s32[512]{0:T(512)S(1)} %get-tuple-element.13.start_ref, s32[512]{0:T(512)S(1)} %get-tuple-element.12.count_ref, bf16[3072,1024]{1,0:T(8,128)(2,1)S(1)} %copy-done), custom_call_target="tpu_custom_call" | custom-call | tf_op jit(solution)/shard_map/pack/pallas_call | solution.py:73
  21.5 153.0 %all_to_all.10 = bf16[128,48,1024]{2,1,0:T(8,128)(2,1)} all-to-all(bf16[128,48,1024]{2,1,0:T(8,128)(2,1)} %bitcast.11), channel_id=1, replica_groups=mesh['node'=8,'outer'=16] {'node','outer'}, dimensions={0} | all-to-all | bytes 25165824 | tf_op jit(solution)/shard_map/all_to_all | solution.py:216
  174.5 12.1 %child_sums.1 = bf16[8,72,1024]{2,1,0:T(8,128)(2,1)S(1)} custom-call(bf16[6144,1024]{1,0:T(8,128)(2,1)} %bitcast.12, bf16[4,128,1024]{2,1,0:T(8,128)(2,1)S(1)} %get-tuple-element.8.low_ref, f32[4,128,1024]{2,1,0:T(8,128)S(1)} %get-tuple-element.9.unit_ref), custom_call_target="tpu_custom_call" | custom-call | tf_op jit(solution)/shard_map/child_sums/pallas_call | solution.py:144
  186.6 20.5 %all_to_all.11 = bf16[8,72,1024]{2,1,0:T(8,128)(2,1)} all-to-all(bf16[8,72,1024]{2,1,0:T(8,128)(2,1)S(1)} %child_sums.1), channel_id=1, replica_groups=mesh['node'=8,'outer'=16] {'node'}, dimensions={0} | all-to-all | bytes 2359296 | tf_op jit(solution)/shard_map/all_to_all | solution.py:226
  207.1 3.6 %put_in_order.1 = (f32[512,1024]{1,0:T(8,128)}, f32[32,1024]{1,0:T(8,128)}) custom-call(bf16[576,1024]{1,0:T(8,128)(2,1)} %bitcast.13), custom_call_target="tpu_custom_call" | custom-call | tf_op jit(solution)/shard_map/put_in_order/pallas_call | solution.py:181
  (1 shorter events, 0.0 us)
Async XLA Ops:
  1.5 4.9 %copy-start = (bf16[3072,1024]{1,0:T(8,128)(2,1)S(1)}, bf16[3072,1024]{1,0:T(8,128)(2,1)}, u32[]{:S(2)}) copy-start(bf16[3072,1024]{1,0:T(8,128)(2,1)} %rows_ref.1) | copy-start | bytes 18874372
  4.2 0.7 copy-start.1

commit v2 on v1

--- a/solution.py
+++ b/solution.py
@@ -18,6 +18,11 @@
 GROUPS = ROWS // TILE
 PAIRS = 4
 WIN = 32
+SHORT = 32
+GUESTS = 2
+DENSE_PAIRS = 4
+LANES = 128
+NOBODY = 64
 
 
 def unit_scale(values):
@@ -189,40 +194,434 @@
     return children.reshape(per_node, slots, width), parents
 
 
+def dense_pack_kernel(
+    outers,
+    owned,
+    plan_ref,
+    spill_ref,
+    rows_ref,
+    common_ref,
+    out_ref,
+    unit_ref,
+):
+    total, width = rows_ref.shape
+    step = pl.program_id(0)
+    chunk = 64
+
+    @pl.when(step == 0)
+    def _():
+        unit_ref[total:, :] = jnp.zeros((unit_ref.shape[0] - total, width), jnp.bfloat16)
+
+        def normalise(i, carry):
+            at = pl.ds(pl.multiple_of(i * chunk, chunk), chunk)
+            unit_ref[at, :] = unit_scale(rows_ref[at, :].astype(jnp.float32)).astype(jnp.bfloat16)
+            return carry
+
+        lax.fori_loop(0, total // chunk, normalise, 0, unroll=4)
+
+    row = lax.broadcasted_iota(jnp.int32, (2 * SHORT, 1), 0)
+    half = lax.shift_right_logical(row, 5)
+    place = (row & (SHORT - 1)) - 1
+    column = lax.broadcasted_iota(jnp.int32, (2 * SHORT, 2 * OWN * WIN), 1)
+    lane = lax.broadcasted_iota(jnp.int32, (1, LANES), 1)
+    lane_place = (lane & (SHORT - 1)) - 1
+    top = lax.broadcasted_iota(jnp.int32, (8, 1), 0) == 0
+    blank = jnp.zeros((1, LANES), jnp.float32)
+    filler = jnp.zeros((1, width - 3 * LANES), jnp.float32)
+    for pair in range(DENSE_PAIRS):
+        target = jnp.full((2 * SHORT, 1), -1, jnp.int32)
+        windows = []
+        heads = []
+        for h in range(2):
+            device = (step * DENSE_PAIRS + pair) * 2 + h
+            base = lax.rem(device, outers) * owned + lax.div(device, outers) * OWN
+            low_end = jnp.int32(0)
+            slots = jnp.full((1, LANES), NOBODY, jnp.int32)
+            for j in range(OWN):
+                start = plan_ref[0, base + j]
+                high_end = jnp.minimum(low_end + plan_ref[1, base + j], SHORT - 1)
+                aligned = lax.shift_left(lax.shift_right_logical(start, 4), 4)
+                windows.append(unit_ref[pl.ds(pl.multiple_of(aligned, TILE), WIN), :])
+                spot = (h * OWN + j) * WIN + (start - aligned) - low_end + place
+                target = jnp.where(
+                    (half == h) & (place >= low_end) & (place < high_end), spot, target
+                )
+                slots = jnp.where((lane_place >= low_end) & (lane_place < high_end), j, slots)
+                low_end = high_end
+            heads.append(
+                jnp.concatenate(
+                    [slots.astype(jnp.float32), common_ref[0:1, :], common_ref[1:2, :], filler],
+                    axis=1,
+                )
+            )
+        selector = (column == target).astype(jnp.float32).astype(jnp.bfloat16)
+        moved = jnp.dot(
+            selector, jnp.concatenate(windows, axis=0), preferred_element_type=jnp.float32
+        )
+        pieces = []
+        for h in range(2):
+            pieces.append(jnp.where(top, heads[h], moved[h * SHORT : h * SHORT + 8]))
+            pieces.append(moved[h * SHORT + 8 : (h + 1) * SHORT])
+        out_ref[pair * 2 * SHORT : (pair + 1) * 2 * SHORT, :] = jnp.concatenate(
+            pieces, axis=0
+        ).astype(jnp.bfloat16)
+
+    tile_row = lax.broadcasted_iota(jnp.int32, (TILE, 1), 0)
+    for m in range(2 * DENSE_PAIRS):
+        device = step * 2 * DENSE_PAIRS + m
+        outer = lax.rem(device, outers)
+        base = outer * owned + lax.div(device, outers) * OWN
+        guests = plan_ref[2, base]
+        for i in range(GUESTS):
+
+            @pl.when(guests > i)
+            def _():
+                entry = plan_ref[3, base] + i * plan_ref[4, base]
+                source = spill_ref[outer, entry]
+                slot = spill_ref[outers + outer, entry].astype(jnp.float32)
+                aligned = lax.shift_left(lax.shift_right_logical(source, 4), 4)
+                tile = unit_ref[pl.ds(pl.multiple_of(aligned, TILE), TILE), :].astype(jnp.float32)
+                chosen = jnp.sum(
+                    jnp.where(tile_row == source - aligned, tile, 0.0), axis=0, keepdims=True
+                )
+                tail = slice(m * SHORT + TILE, (m + 1) * SHORT)
+                kept = out_ref[tail, :].astype(jnp.float32)
+                out_ref[tail, :] = jnp.where(tile_row == TILE - 1 - i, chosen, kept).astype(
+                    jnp.bfloat16
+                )
+                head = slice(m * SHORT, m * SHORT + TILE)
+                where = slice(3 * LANES, 4 * LANES)
+                kept = out_ref[head, where].astype(jnp.float32)
+                mine = (tile_row == 0) & ((lane & 7) == 7 - i)
+                out_ref[head, where] = jnp.where(mine, slot, kept).astype(jnp.bfloat16)
+
+
+def dense_pack(embeddings, scalars, common, outers, owned, devices):
+    total, width = embeddings.shape
+    block = 2 * SHORT * DENSE_PAIRS
+    return pl.pallas_call(
+        functools.partial(dense_pack_kernel, outers, owned),
+        out_shape=jax.ShapeDtypeStruct((devices * SHORT, width), jnp.bfloat16),
+        grid_spec=pltpu.PrefetchScalarGridSpec(
+            num_scalar_prefetch=len(scalars),
+            grid=(devices // (2 * DENSE_PAIRS),),
+            in_specs=[
+                pl.BlockSpec((total, width), lambda i, *_: (0, 0), pipeline_mode=pl.Buffered(1)),
+                pl.BlockSpec((2, LANES), lambda i, *_: (0, 0), pipeline_mode=pl.Buffered(1)),
+            ],
+            out_specs=pl.BlockSpec((block, width), lambda i, *_: (i, 0)),
+            scratch_shapes=[pltpu.VMEM((total + WIN, width), jnp.bfloat16)],
+        ),
+        compiler_params=pltpu.CompilerParams(vmem_limit_bytes=54 << 20),
+        name="dense_pack",
+    )(*scalars, embeddings, common)
+
+
+def collect_kernel(me_ref, rows_ref, head_ref, late_ref, notes_ref, unfit_ref, wide_ref):
+    sources = rows_ref.shape[0]
+    width = rows_ref.shape[2]
+    columns = sources * 8
+    heads = head_ref[...].astype(jnp.float32).reshape(sources * 8, head_ref.shape[2])
+    notes = []
+    for q in range(wide_ref.shape[0]):
+        wide_ref[q] = heads[:, q * LANES : (q + 1) * LANES]
+        notes.append(wide_ref[q, pl.ds(0, sources, stride=8), :])
+    notes = jnp.concatenate(notes, axis=1)
+    notes_ref[...] = notes[:, :LANES]
+    everyone = notes[:, LANES : 2 * LANES]
+    crowded = jnp.max(jnp.sum(everyone, axis=0, keepdims=True)) > SHORT - 1
+    failed = jnp.max(notes[:, 2 * LANES : 3 * LANES]) > 0.0
+    unfit_ref[0] = (crowded | failed).astype(jnp.int32)
+
+    lane = lax.broadcasted_iota(jnp.int32, (1, LANES), 1)
+    guests = jnp.sum(jnp.where(lane == me_ref[0], everyone, 0.0), axis=1, keepdims=True)
+    column = lax.broadcasted_iota(jnp.int32, (1, columns), 1)
+    owner = lax.shift_right_logical(column, 3)
+    source = lax.broadcasted_iota(jnp.int32, (sources, 1), 0)
+    before = jnp.sum(jnp.where(source < owner, guests, 0.0), axis=0, keepdims=True)
+    here = jnp.sum(jnp.where(source == owner, guests, 0.0), axis=0, keepdims=True)
+    slots = jnp.concatenate([notes[:, 3 * LANES :]] * (columns // LANES), axis=1)
+    slots = jnp.sum(jnp.where(source == owner, slots, 0.0), axis=0, keepdims=True)
+    order = 7 - (column & 7)
+    place = jnp.where(order < here.astype(jnp.int32), before.astype(jnp.int32) + order + 1, -1)
+    wanted = lax.broadcasted_iota(jnp.int32, (LANES, 1), 0) & (SHORT - 1)
+    selector = (wanted == place).astype(jnp.float32).astype(jnp.bfloat16)
+    slots = jnp.broadcast_to(slots, (8, columns)).astype(jnp.bfloat16)
+    head = lax.dot_general(
+        slots, selector, (((1,), (1,)), ((), ())), preferred_element_type=jnp.float32
+    )[0:1]
+    head = jnp.concatenate([head] * (width // LANES), axis=1)
+    rows = rows_ref[...].astype(jnp.float32).reshape(columns, width).astype(jnp.bfloat16)
+    moved = jnp.dot(selector[:SHORT], rows, preferred_element_type=jnp.float32)
+    top = lax.broadcasted_iota(jnp.int32, (SHORT, 1), 0) == 0
+    moved = jnp.where(top, head, moved).astype(jnp.bfloat16)
+    for n in range(late_ref.shape[0]):
+        late_ref[n] = moved
+
+
+def collect(arrived, me, nodes):
+    sources, short, width = arrived.shape
+    return pl.pallas_call(
+        collect_kernel,
+        out_shape=(
+            jax.ShapeDtypeStruct((nodes, SHORT, width), jnp.bfloat16),
+            jax.ShapeDtypeStruct((sources, LANES), jnp.float32),
+            jax.ShapeDtypeStruct((1,), jnp.int32),
+        ),
+        grid_spec=pltpu.PrefetchScalarGridSpec(
+            num_scalar_prefetch=1,
+            grid=(1,),
+            in_specs=[
+                pl.BlockSpec((sources, 8, width), lambda i, m: (0, short // 8 - 1, 0)),
+                pl.BlockSpec((sources, 8, 4 * LANES), lambda i, m: (0, 0, 0)),
+            ],
+            out_specs=(
+                pl.BlockSpec((nodes, SHORT, width), lambda i, m: (0, 0, 0)),
+                pl.BlockSpec((sources, LANES), lambda i, m: (0, 0)),
+                pl.BlockSpec(memory_space=pltpu.SMEM),
+            ),
+            scratch_shapes=[pltpu.VMEM((4, sources * 8, LANES), jnp.float32)],
+        ),
+        compiler_params=pltpu.CompilerParams(vmem_limit_bytes=58 << 20),
+        name="collect",
+    )(me, arrived, arrived)
+
+
+def weighted_rows(low, rows, slots, shrink):
+    children = low.shape[0] // OWN
+    logits = lax.dot_general(
+        low, rows, (((1,), (1,)), ((), ())), preferred_element_type=jnp.float32
+    )
+    chosen = jnp.zeros((children, rows.shape[0]), jnp.float32)
+    for j in range(OWN):
+        chosen = jnp.where(slots == j, logits[j * children : (j + 1) * children], chosen)
+    raised = jnp.exp(chosen * shrink)
+    weights = raised / jnp.sum(raised, axis=0, keepdims=True)
+    spread = jnp.concatenate(
+        [jnp.where(slots == j, weights, 0.0) for j in range(OWN)], axis=0
+    ).astype(jnp.bfloat16)
+    return jnp.dot(spread, rows, preferred_element_type=jnp.float32)
+
+
+def along_lanes(notes):
+    count = notes.shape[0]
+    column = lax.broadcasted_iota(jnp.int32, (1, count * SHORT), 1)
+    source = lax.broadcasted_iota(jnp.int32, (count, 1), 0)
+    wide = jnp.concatenate([notes] * (count * SHORT // LANES), axis=1)
+    mine = source == lax.shift_right_logical(column, 5)
+    return jnp.sum(jnp.where(mine, wide, 0.0), axis=0, keepdims=True).astype(jnp.int32)
+
+
+def dense_sums_kernel(shrink, rows_ref, notes_ref, low_ref, total_ref):
+    sums = weighted_rows(low_ref[...], rows_ref[...], along_lanes(notes_ref[...]), shrink)
+
+    @pl.when(pl.program_id(0) == 0)
+    def _():
+        total_ref[...] = sums
+
+    @pl.when(pl.program_id(0) > 0)
+    def _():
+        total_ref[...] += sums
+
+
+def dense_sums(arrived, notes, low, shrink):
+    total, width = arrived.shape
+    block = 32 * SHORT
+    return pl.pallas_call(
+        functools.partial(dense_sums_kernel, shrink),
+        out_shape=jax.ShapeDtypeStruct(low.shape, jnp.float32),
+        grid=(total // block,),
+        in_specs=[
+            pl.BlockSpec((block, width), lambda i: (i, 0)),
+            pl.BlockSpec((block // SHORT, LANES), lambda i: (i, 0)),
+            pl.BlockSpec(low.shape, lambda i: (0, 0), pipeline_mode=pl.Buffered(1)),
+        ],
+        out_specs=pl.BlockSpec(low.shape, lambda i: (0, 0)),
+        compiler_params=pltpu.CompilerParams(vmem_limit_bytes=48 << 20),
+        cost_estimate=pl.CostEstimate(
+            flops=4 * total * width * low.shape[0],
+            bytes_accessed=2 * total * width + 6 * low.size,
+            transcendentals=total * low.shape[0] // OWN,
+        ),
+        name="dense_sums",
+    )(arrived, notes, low)
+
+
+def finish_kernel(shrink, per_node, node_ref, total_ref, late_ref, low_ref, unit_ref, out_ref):
+    children = unit_ref.shape[1]
+    late = late_ref.shape[0] // SHORT
+    notes = jnp.concatenate(
+        [
+            late_ref[b * SHORT : b * SHORT + TILE, :LANES].astype(jnp.float32)[0:1]
+            for b in range(late)
+        ],
+        axis=0,
+    )
+    slots = along_lanes(notes) - 1 - OWN * node_ref[0]
+    added = weighted_rows(low_ref[...], late_ref[...], slots, shrink)
+    parents = []
+    for j in range(OWN):
+        at = slice(j * children, (j + 1) * children)
+        fresh = unit_scale(prior_weight * unit_ref[j] + (total_ref[at, :] + added[at]))
+        parents.append(unit_scale(jnp.sum(fresh, axis=0, keepdims=True)))
+        fresh = fresh.astype(jnp.bfloat16)
+        for m in range(children // per_node):
+            out_ref[m, j * per_node : (j + 1) * per_node, :] = fresh[
+                m * per_node : (m + 1) * per_node
+            ]
+    tail = jnp.concatenate(parents + parents, axis=0).astype(jnp.bfloat16)
+    for m in range(children // per_node):
+        out_ref[m, OWN * per_node :, :] = tail
+
+
+def finish(total, late, low, unit, node, shrink, nodes):
+    per_node = unit.shape[1] // nodes
+    out = (nodes, OWN * per_node + 2 * OWN, late.shape[1])
+    return pl.pallas_call(
+        functools.partial(finish_kernel, shrink, per_node),
+        out_shape=jax.ShapeDtypeStruct(out, jnp.bfloat16),
+        in_specs=[pl.BlockSpec(memory_space=pltpu.SMEM)]
+        + [pl.BlockSpec(memory_space=pltpu.VMEM)] * 4,
+        compiler_params=pltpu.CompilerParams(vmem_limit_bytes=48 << 20),
+        name="finish",
+    )(node, total, late, low, unit)
+
+
+def plan_kernel(outers, nodes, rank_ref, slot_ref, ids_ref, plan_ref, spill_ref, common_ref):
+    slots = slot_ref.shape[1]
+    owned = slots // outers
+    room = SHORT - 1
+    row = lax.broadcasted_iota(jnp.int32, (slots, 1), 0)
+    other = lax.broadcasted_iota(jnp.int32, (1, slots), 1)
+    lane = lax.broadcasted_iota(jnp.int32, (1, LANES), 1)
+    parent = jnp.sum(
+        jnp.where(slot_ref[...] == row, other.astype(jnp.float32), 0.0), axis=1, keepdims=True
+    ).astype(jnp.int32)
+    ids = ids_ref[...]
+    starts = []
+    counts = []
+    for at in range(0, slots, 64):
+        mine = parent[at : at + 64]
+        below = jnp.where(ids < mine, 1.0, 0.0)
+        equal = jnp.where(ids == mine, 1.0, 0.0)
+        starts.append(jnp.sum(below, axis=1, keepdims=True))
+        counts.append(jnp.sum(equal, axis=1, keepdims=True))
+    starts = jnp.concatenate(starts, axis=0)
+    counts = jnp.concatenate(counts, axis=0)
+
+    def total(mask, columns):
+        wide = jnp.zeros((slots, LANES), jnp.float32)
+        for q, value in enumerate(columns):
+            wide = jnp.where(lane == q, value, wide)
+        mask = mask.astype(jnp.float32).astype(jnp.bfloat16)
+        sums = jnp.dot(mask, wide.astype(jnp.bfloat16), preferred_element_type=jnp.float32)
+        return [sums[:, q : q + 1] for q in range(len(columns))]
+
+    group = lax.shift_right_logical(row, 2)
+    other_group = lax.shift_right_logical(other, 2)
+    outer = lax.div(row, owned)
+    other_outer = lax.div(other, owned)
+    (first,) = total((group == other_group) & (other < row), [counts])
+    (sent,) = total(group == other_group, [counts])
+    over = jnp.maximum(sent - room, 0.0)
+    host = jnp.where(sent <= room - GUESTS, 1.0, 0.0)
+    once = jnp.where((row & (OWN - 1)) == 0, 1.0, 0.0)
+    parts = [over * once, host * once]
+    over_first, host_first = total((outer == other_outer) & (other_group < group), parts)
+    overs, real_hosts = total(outer == other_outer, parts)
+    hosts = jnp.maximum(real_hosts, 1.0)
+    shift = jnp.zeros_like(hosts)
+    for h in range(1, nodes + 1):
+        shift = jnp.where(hosts == h, lax.rem(rank_ref[0], h).astype(jnp.float32), shift)
+    turn = host_first - shift
+    turn = jnp.where(turn < 0.0, turn + hosts, turn)
+    guests = host * (
+        jnp.where(overs > turn, 1.0, 0.0) + jnp.where(overs > turn + hosts, 1.0, 0.0)
+    )
+    failed = jnp.max(overs - GUESTS * real_hosts) > 0.0
+
+    wide = jnp.zeros((slots, LANES), jnp.float32)
+    for q, value in enumerate([starts, counts, guests, turn, hosts]):
+        wide = jnp.where(lane == q, value, wide)
+    plan_ref[...] = jnp.transpose(wide)[:8].astype(jnp.int32)
+
+    begin = over_first + jnp.maximum(first - room, 0.0)
+    end = over_first + jnp.maximum(first + counts - room, 0.0)
+    entry = lane.astype(jnp.float32)
+    held = (begin <= entry) & (entry < end)
+    source = jnp.where(held, starts - first + room - over_first + entry, 0.0)
+    named = jnp.where(held, ((row & (owned - 1)) + 1).astype(jnp.float32), 0.0)
+    for o in range(outers):
+        at = slice(o * owned, (o + 1) * owned)
+        spill_ref[o : o + 1, :] = jnp.sum(source[at], axis=0, keepdims=True).astype(jnp.int32)
+        spill_ref[outers + o : outers + o + 1, :] = jnp.sum(
+            named[at], axis=0, keepdims=True
+        ).astype(jnp.int32)
+    where = (lane & (outers - 1)) * owned + lax.div(lane, outers) * OWN
+    common_ref[0:1, :] = jnp.sum(jnp.where(row == where, guests, 0.0), axis=0, keepdims=True)
+    common_ref[1:2, :] = jnp.broadcast_to(failed.astype(jnp.float32), (1, LANES))
+
+
+def plan(parent_slot, embedding_parent_index, rank, outers, nodes):
+    slots = parent_slot.shape[0]
+    return pl.pallas_call(
+        functools.partial(plan_kernel, outers, nodes),
+        out_shape=(
+            jax.ShapeDtypeStruct((8, slots), jnp.int32),
+            jax.ShapeDtypeStruct((2 * outers, LANES), jnp.int32),
+            jax.ShapeDtypeStruct((2, LANES), jnp.float32),
+        ),
+        in_specs=[pl.BlockSpec(memory_space=pltpu.SMEM)]
+        + [pl.BlockSpec(memory_space=pltpu.VMEM)] * 2,
+        name="plan",
+    )(rank, parent_slot.reshape(1, -1), embedding_parent_index.reshape(1, -1))
+
+
 def body(embeddings, embedding_parent_index, parent_slot, centroids):
     width = embeddings.shape[1]
     children, owned, _ = centroids.shape
-    parent_count = parent_slot.shape[0]
     nodes = lax.axis_size("node")
     outers = lax.axis_size("outer")
     devices = nodes * outers
     shrink = 1.0 / (softness_level * width)
     node = lax.axis_index("node")
-
-    ids = jnp.arange(parent_count, dtype=jnp.int32)
-    held = (parent_slot[None, :] == ids[:, None]).astype(jnp.int32)
-    parent_of_slot = jnp.sum(held * ids[None, :], axis=1)
-    starts = jnp.sum(
-        (embedding_parent_index[None, :] < parent_of_slot[:, None]).astype(jnp.int32), axis=1
-    )
-    counts = jnp.sum(
-        (embedding_parent_index[None, :] == parent_of_slot[:, None]).astype(jnp.int32), axis=1
-    )
+    everyone = ("node", "outer")
+    rank = lax.axis_index(everyone)
+
     own = lax.dynamic_slice_in_dim(centroids, node * OWN, OWN, 1).transpose(1, 0, 2)
     unit = unit_scale(own.astype(jnp.float32))
     low = unit.astype(jnp.bfloat16)
-    packed = pack(embeddings, starts, counts, outers, owned, devices)
-    packed, unit, low = lax.optimization_barrier((packed, unit, low))
+    places, spill, common = plan(
+        parent_slot, embedding_parent_index, rank.reshape(1), outers, nodes
+    )
+    packed = dense_pack(embeddings, (places, spill), common, outers, owned, devices)
+    packed, unit, low, embeddings, places, me, here = lax.optimization_barrier(
+        (packed, unit, low, embeddings, places, rank.reshape(1), node.reshape(1))
+    )
     arrived = lax.all_to_all(
-        packed.reshape(devices, ROWS, width),
-        ("node", "outer"),
-        split_axis=0,
-        concat_axis=0,
-        tiled=True,
-    )
-    fresh = child_sums(
-        arrived.reshape(devices * ROWS, width), low, unit, shrink, nodes
-    )
+        packed.reshape(devices, SHORT, width), everyone, split_axis=0, concat_axis=0, tiled=True
+    )
+    late, notes, unfit = collect(arrived, me, nodes)
+    unfit, unit, low, embeddings, places, here = lax.optimization_barrier(
+        (unfit, unit, low, embeddings, places, here)
+    )
+
+    def short_way():
+        arrivals = lax.all_to_all(late, "node", split_axis=0, concat_axis=0, tiled=True)
+        flat = low.reshape(OWN * children, width)
+        total = dense_sums(arrived.reshape(devices * SHORT, width), notes, flat, shrink)
+        return finish(
+            total, arrivals.reshape(nodes * SHORT, width), flat, unit, here, shrink, nodes
+        )
+
+    def long_way():
+        full = pack(embeddings, places[0], places[1], outers, owned, devices)
+        full = lax.all_to_all(
+            full.reshape(devices, ROWS, width), everyone, split_axis=0, concat_axis=0, tiled=True
+        )
+        return child_sums(full.reshape(devices * ROWS, width), low, unit, shrink, nodes)
+
+    fresh = lax.cond(unfit[0] > 0, long_way, short_way)
     received = lax.all_to_all(fresh, "node", split_axis=0, concat_axis=0, tiled=True)
     return put_in_order(received, children // nodes)
 

time: 211 us -> 187 us (0.89)
  blocking collectives: 174 us -> 130 us
  Pallas kernels: 30.8 us -> 47.6 us
  starting transfers between devices: 0 us -> 4.13 us
    all_to_all x1, blocking collectives: 153 us -> 108 us  [body(): lax.all_to_all(packed.reshape(devices, SHORT, width), everyone, split_axi...]
    pallas_call x2 -> x5, Pallas kernels: 27.1 us -> 43.9 us  [the longest x1 19 us: dense_pack(): pl.pallas_call(functools.partial(dense_pack_kernel, outers, owned), out_s...]
    all_to_all x0 -> x1, starting transfers between devices: none -> 4.13 us  [short_way(): lax.all_to_all(late, 'node', split_axis=0, concat_axis=0, tiled=True)]
    reduce_sum x2 -> x0, other arithmetic: 2.36 us -> none  [the longest x1 1.49 us: body(): jnp.sum((embedding_parent_index[None, :] == parent_of_slot[:, None]).asty...]
  transfers between devices with their start and end apart: 0 -> 1, of which waited for: 0 -> 0; matrix products, arithmetic and copies ran while one was open for 0% -> 0% of each run, Pallas kernels for 0% -> 7%
where the time goes in v2:
time: 187 us
  blocking collectives  130 us (70%)
  Pallas kernels  47.6 us (25%)
  starting transfers between devices  4.13 us (2%)
  local copies, waits for them, and re-layouts  2.15 us (1%)
  other arithmetic  2.12 us (1%)
    all_to_all x1, blocking collectives, body(): lax.all_to_all(packed.reshape(devices, SHORT, width), everyone, split_axi...  108 us
    all_to_all x1, blocking collectives, body(): lax.all_to_all(fresh, 'node', split_axis=0, concat_axis=0, tiled=True)  21.4 us
    pallas_call x1, Pallas kernels, dense_pack(): pl.pallas_call(functools.partial(dense_pack_kernel, outers, owned), out_s...  19 us
    pallas_call x1, Pallas kernels, dense_sums(): pl.pallas_call(functools.partial(dense_sums_kernel, shrink), out_shape=ja...  12.2 us
    pallas_call x1, Pallas kernels, finish(): pl.pallas_call(functools.partial(finish_kernel, shrink, per_node), out_sh...  4.82 us
    pallas_call x1, Pallas kernels, plan(): pl.pallas_call(functools.partial(plan_kernel, outers, nodes), out_shape=(...  4.54 us
    all_to_all x1, starting transfers between devices, short_way(): lax.all_to_all(late, 'node', split_axis=0, concat_axis=0, tiled=True)  4.13 us
  transfers between devices with their start and end apart: 1, of which 0 were waited for; matrix products, arithmetic and copies ran while one was open for 0% of the time, Pallas kernels for 7%

profile of v2, /device:TPU:1, one launch (start us, length us, event | category | flops | bytes accessed | tf_op | source)
XLA Modules:
  0.0 186.9 jit_solution(4632169178689596586)
XLA Ops:
  0.6 2.1 %constant_dynamic-slice_fusion = bf16[128,4,1024]{2,1,0:T(4,128)(2,1)S(1)} fusion(bf16[128,32,1024]{2,1,0:T(8,128)(2,1)} %param.9, s32[]{:T(128)S(6)} %select_n.3), kind=kLoop, calls=%fused_computation.5 | loop fusion | bytes 2097156 | tf_op jit(solution)/shard_map/dynamic_slice | solution.py:591
  2.8 0.4 fusion
  3.2 1.7 fusion.1
  4.9 4.5 %plan.1 = (s32[8,512]{1,0:T(8,128)S(1)}, s32[32,128]{1,0:T(8,128)}, f32[2,128]{1,0:T(2,128)}) custom-call(s32[1]{0:T(128)} %bitcast.7.rank_ref.me_ref, s32[1,512]{1,0:T(1,128)} %bitcast.33, s32[1,3072]{1,0:T(1,128)} %bitcast.32), custom_call_target="tpu_custom_call" | custom-call | tf_op jit(solution)/shard_map/plan/pallas_call | solution.py:567
  9.4 19.0 %dense_pack.1 = bf16[4096,1024]{1,0:T(8,128)(2,1)} custom-call(s32[8,512]{1,0:T(8,128)S(1)} %get-tuple-element.73.plan_ref, s32[32,128]{1,0:T(8,128)} %get-tuple-element.57.spill_ref, bf16[3072,1024]{1,0:T(8,128)(2,1)} %rows_ref.1, f32[2,128]{1,0:T(2,128)} %get-tuple-element.58.common_ref), custom_call_target="tpu_custom_call" | custom-call | tf_op jit(solution)/shard_map/dense_pack/pallas_call | solution.py:302
  28.4 108.2 %all_to_all.19.rows_ref.head_ref = bf16[128,32,1024]{2,1,0:T(8,128)(2,1)} all-to-all(bf16[128,32,1024]{2,1,0:T(8,128)(2,1)} %bitcast.28), channel_id=1, replica_groups=mesh['node'=8,'outer'=16] {'node','outer'}, dimensions={0} | all-to-all | bytes 16777216 | tf_op jit(solution)/shard_map/all_to_all | solution.py:601
  136.6 3.4 %collect.1 = (bf16[8,32,1024]{2,1,0:T(8,128)(2,1)}, f32[128,128]{1,0:T(8,128)S(1)}, s32[1]{0:T(128)}) custom-call(s32[1]{0:T(128)} %bitcast.7.rank_ref.me_ref, bf16[128,32,1024]{2,1,0:T(8,128)(2,1)} %all_to_all.19.rows_ref.head_ref, bf16[128,32,1024]{2,1,0:T(8,128)(2,1)} %all_to_all.19.rows_ref.head_ref), custom_call_target="tpu_custom_call" | custom-call | tf_op jit(solution)/shard_map/collect/pallas_call | solution.py:364
  140.7 21.2 %conditional.1 = (bf16[8,72,1024]{2,1,0:T(8,128)(2,1)}) conditional(s32[]{:T(128)} %bitcast.13, (bf16[128,32,1024]{2,1,0:T(8,128)(2,1)}, bf16[4,128,1024]{2,1,0:T(8,128)(2,1)S(1)}, f32[128,128]{1,0:T(8,128)S(1)}, bf16[8,32,1024]{2,1,0:T(8,128)(2,1)}, s32[1]{0:T(128)}, /*index=5*/f32[4,128,1024]{2,1,0:T(8,128)}) %tuple.18, (s32[8,512]{1,0:T(8,128)S(1)}, ...), branch_computations={%region_1.0_spmd, %region_2.0_spmd} | conditional | flops 8589934592 | bytes 41951324 | solution.py:624
  140.7 0.0 copy-start.1
  140.7 4.1 %all-to-all-start = ((bf16[8,32,1024]{2,1,0:T(8,128)(2,1)}), bf16[8,32,1024]{2,1,0:T(8,128)(2,1)S(1)}, u32[]{:S(2)}, u32[]{:S(2)}) async-start(bf16[8,32,1024]{2,1,0:T(8,128)(2,1)} %get-tuple-element.27), calls=%async_computation | async-start | bytes 1048576 | tf_op jit(solution)/shard_map/cond/branch_0_fun/all_to_all | solution.py:610
  144.8 0.0 copy-done.1
  144.8 12.2 %dense_sums.1.total_ref = f32[512,1024]{1,0:T(8,128)S(1)} custom-call(bf16[4096,1024]{1,0:T(8,128)(2,1)} %bitcast.26, f32[128,128]{1,0:T(8,128)S(1)} %get-tuple-element.25.notes_ref, bf16[512,1024]{1,0:T(8,128)(2,1)} %bitcast.29), custom_call_target="tpu_custom_call" | custom-call | flops 8589934592 | bytes 11534336 | tf_op jit(solution)/shard_map/cond/branch_0_fun/dense_sums/pallas_call | solution.py:430
  157.0 0.0 all-to-all-done
  157.0 4.8 %finish.1 = bf16[8,72,1024]{2,1,0:T(8,128)(2,1)} custom-call(s32[1]{0:T(128)} %get-tuple-element.15.node_ref, f32[512,1024]{1,0:T(8,128)S(1)} %dense_sums.1.total_ref, bf16[256,1024]{1,0:T(8,128)(2,1)S(1)} %bitcast.23, bf16[512,1024]{1,0:T(8,128)(2,1)} %bitcast.30, f32[4,128,1024]{2,1,0:T(8,128)} %get-tuple-element.28.unit_ref), custom_call_target="tpu_custom_call" | custom-call | tf_op jit(solution)/shard_map/cond/branch_0_fun/finish/pallas_call | solution.py:480
  161.9 21.4 %all_to_all.20 = bf16[8,72,1024]{2,1,0:T(8,128)(2,1)} all-to-all(bf16[8,72,1024]{2,1,0:T(8,128)(2,1)} %get-tuple-element.81), channel_id=1, replica_groups=mesh['node'=8,'outer'=16] {'node'}, dimensions={0} | all-to-all | bytes 2359296 | tf_op jit(solution)/shard_map/all_to_all | solution.py:625
  183.3 3.6 %put_in_order.1 = (f32[512,1024]{1,0:T(8,128)}, f32[32,1024]{1,0:T(8,128)}) custom-call(bf16[576,1024]{1,0:T(8,128)(2,1)} %bitcast.31), custom_call_target="tpu_custom_call" | custom-call | tf_op jit(solution)/shard_map/put_in_order/pallas_call | solution.py:186
  (1 shorter events, 0.0 us)
Async XLA Ops:
  140.7 4.1 %copy-start.1 = (bf16[4,128,1024]{2,1,0:T(8,128)(2,1)}, bf16[4,128,1024]{2,1,0:T(8,128)(2,1)S(1)}, u32[]{:S(2)}) copy-start(bf16[4,128,1024]{2,1,0:T(8,128)(2,1)S(1)} %get-tuple-element.26) | copy-start | bytes 3145732 | tf_op jit(solution)/shard_map/cond
  140.7 16.3 %all-to-all-start = ((bf16[8,32,1024]{2,1,0:T(8,128)(2,1)}), bf16[8,32,1024]{2,1,0:T(8,128)(2,1)S(1)}, u32[]{:S(2)}, u32[]{:S(2)}) async-start(bf16[8,32,1024]{2,1,0:T(8,128)(2,1)} %get-tuple-element.27), calls=%async_computation | async-start | bytes 1048576 | tf_op jit(solution)/shard_map/cond/branch_0_fun/all_to_all | solution.py:610

commit v3 on v2

--- a/solution.py
+++ b/solution.py
@@ -20,7 +20,7 @@
 WIN = 32
 SHORT = 32
 GUESTS = 2
-DENSE_PAIRS = 4
+DENSE_PAIRS = 8
 LANES = 128
 NOBODY = 64
 
@@ -197,66 +197,71 @@
 def dense_pack_kernel(
     outers,
     owned,
-    plan_ref,
+    start_ref,
+    count_ref,
+    guests_ref,
+    turn_ref,
+    hosts_ref,
     spill_ref,
+    node_ref,
     rows_ref,
     common_ref,
+    centroid_ref,
     out_ref,
+    low_ref,
     unit_ref,
+    wide_ref,
 ):
     total, width = rows_ref.shape
     step = pl.program_id(0)
-    chunk = 64
-
-    @pl.when(step == 0)
-    def _():
-        unit_ref[total:, :] = jnp.zeros((unit_ref.shape[0] - total, width), jnp.bfloat16)
-
-        def normalise(i, carry):
-            at = pl.ds(pl.multiple_of(i * chunk, chunk), chunk)
-            unit_ref[at, :] = unit_scale(rows_ref[at, :].astype(jnp.float32)).astype(jnp.bfloat16)
-            return carry
-
-        lax.fori_loop(0, total // chunk, normalise, 0, unroll=4)
-
-    row = lax.broadcasted_iota(jnp.int32, (2 * SHORT, 1), 0)
-    half = lax.shift_right_logical(row, 5)
-    place = (row & (SHORT - 1)) - 1
-    column = lax.broadcasted_iota(jnp.int32, (2 * SHORT, 2 * OWN * WIN), 1)
+    outer_bits = outers.bit_length() - 1
+    centroids = centroid_ref[...].astype(jnp.float32).reshape(wide_ref.shape[1], width)
+    for c in range(width // LANES):
+        wide_ref[c] = centroids[:, c * LANES : (c + 1) * LANES]
+    for j in range(OWN):
+        at = OWN * (node_ref[0] & 1) + j
+        few = wide_ref.shape[1] // 8
+        mine = [wide_ref[c, pl.ds(at, few, stride=8), :] for c in range(width // LANES)]
+        unit = unit_scale(jnp.concatenate(mine, axis=1))
+        unit_ref[j] = unit
+        low_ref[j] = unit.astype(jnp.bfloat16)
+
+    place = lax.broadcasted_iota(jnp.int32, (SHORT, 1), 0) - 1
+    column = lax.broadcasted_iota(jnp.int32, (SHORT, 2 * OWN * WIN), 1)
     lane = lax.broadcasted_iota(jnp.int32, (1, LANES), 1)
     lane_place = (lane & (SHORT - 1)) - 1
     top = lax.broadcasted_iota(jnp.int32, (8, 1), 0) == 0
-    blank = jnp.zeros((1, LANES), jnp.float32)
     filler = jnp.zeros((1, width - 3 * LANES), jnp.float32)
+    notes = jnp.concatenate([common_ref[0:1, :], common_ref[1:2, :], filler], axis=1)
     for pair in range(DENSE_PAIRS):
-        target = jnp.full((2 * SHORT, 1), -1, jnp.int32)
         windows = []
+        selectors = []
         heads = []
         for h in range(2):
             device = (step * DENSE_PAIRS + pair) * 2 + h
-            base = lax.rem(device, outers) * owned + lax.div(device, outers) * OWN
-            low_end = jnp.int32(0)
+            base = (device & (outers - 1)) * owned + (device >> outer_bits) * OWN
+            at = jnp.int32(0)
+            target = jnp.full((SHORT, 1), -1, jnp.int32)
             slots = jnp.full((1, LANES), NOBODY, jnp.int32)
             for j in range(OWN):
-                start = plan_ref[0, base + j]
-                high_end = jnp.minimum(low_end + plan_ref[1, base + j], SHORT - 1)
+                start = start_ref[base + j]
                 aligned = lax.shift_left(lax.shift_right_logical(start, 4), 4)
-                windows.append(unit_ref[pl.ds(pl.multiple_of(aligned, TILE), WIN), :])
-                spot = (h * OWN + j) * WIN + (start - aligned) - low_end + place
-                target = jnp.where(
-                    (half == h) & (place >= low_end) & (place < high_end), spot, target
-                )
-                slots = jnp.where((lane_place >= low_end) & (lane_place < high_end), j, slots)
-                low_end = high_end
-            heads.append(
-                jnp.concatenate(
-                    [slots.astype(jnp.float32), common_ref[0:1, :], common_ref[1:2, :], filler],
-                    axis=1,
-                )
+                aligned = jnp.minimum(aligned, total - WIN)
+                windows.append(rows_ref[pl.ds(pl.multiple_of(aligned, TILE), WIN), :])
+                spot = (h * OWN + j) * WIN + (start - aligned) - at
+                target = jnp.where(place >= at, place + spot, target)
+                slots = jnp.where(lane_place >= at, j, slots)
+                at = at + count_ref[base + j]
+            target = jnp.where(place < at, target, -1)
+            slots = jnp.where(lane_place < at, slots, NOBODY)
+            selectors.append(jnp.where(column == target, 1.0, 0.0).astype(jnp.bfloat16))
+            heads.append(jnp.concatenate([slots.astype(jnp.float32), notes], axis=1))
+        moved = unit_scale(
+            jnp.dot(
+                jnp.concatenate(selectors, axis=0),
+                jnp.concatenate(windows, axis=0),
+                preferred_element_type=jnp.float32,
             )
-        selector = (column == target).astype(jnp.float32).astype(jnp.bfloat16)
-        moved = jnp.dot(
-            selector, jnp.concatenate(windows, axis=0), preferred_element_type=jnp.float32
         )
         pieces = []
         for h in range(2):
@@ -267,54 +272,78 @@
         ).astype(jnp.bfloat16)
 
     tile_row = lax.broadcasted_iota(jnp.int32, (TILE, 1), 0)
-    for m in range(2 * DENSE_PAIRS):
+
+    def base_of(m):
         device = step * 2 * DENSE_PAIRS + m
-        outer = lax.rem(device, outers)
-        base = outer * owned + lax.div(device, outers) * OWN
-        guests = plan_ref[2, base]
+        return (device & (outers - 1)) * owned + (device >> outer_bits) * OWN
+
+    def seat(m, carry):
+        base = base_of(m)
+        outer = lax.div(base, owned)
         for i in range(GUESTS):
 
-            @pl.when(guests > i)
+            @pl.when(guests_ref[base] > i)
             def _():
-                entry = plan_ref[3, base] + i * plan_ref[4, base]
+                entry = turn_ref[base] + i * hosts_ref[base]
                 source = spill_ref[outer, entry]
                 slot = spill_ref[outers + outer, entry].astype(jnp.float32)
                 aligned = lax.shift_left(lax.shift_right_logical(source, 4), 4)
-                tile = unit_ref[pl.ds(pl.multiple_of(aligned, TILE), TILE), :].astype(jnp.float32)
-                chosen = jnp.sum(
-                    jnp.where(tile_row == source - aligned, tile, 0.0), axis=0, keepdims=True
+                tile = rows_ref[pl.ds(pl.multiple_of(aligned, TILE), TILE), :].astype(jnp.float32)
+                chosen = unit_scale(
+                    jnp.sum(
+                        jnp.where(tile_row == source - aligned, tile, 0.0), axis=0, keepdims=True
+                    )
                 )
-                tail = slice(m * SHORT + TILE, (m + 1) * SHORT)
+                tail = pl.ds(pl.multiple_of(m * SHORT + TILE, TILE), TILE)
                 kept = out_ref[tail, :].astype(jnp.float32)
                 out_ref[tail, :] = jnp.where(tile_row == TILE - 1 - i, chosen, kept).astype(
                     jnp.bfloat16
                 )
-                head = slice(m * SHORT, m * SHORT + TILE)
+                head = pl.ds(pl.multiple_of(m * SHORT, TILE), TILE)
                 where = slice(3 * LANES, 4 * LANES)
                 kept = out_ref[head, where].astype(jnp.float32)
                 mine = (tile_row == 0) & ((lane & 7) == 7 - i)
                 out_ref[head, where] = jnp.where(mine, slot, kept).astype(jnp.bfloat16)
 
-
-def dense_pack(embeddings, scalars, common, outers, owned, devices):
+        return carry
+
+    seated = guests_ref[base_of(0)]
+    for m in range(1, 2 * DENSE_PAIRS):
+        seated = seated + guests_ref[base_of(m)]
+
+    @pl.when(seated > 0)
+    def _():
+        lax.fori_loop(0, 2 * DENSE_PAIRS, seat, 0)
+
+
+def dense_pack(embeddings, scalars, common, centroids, outers, devices):
     total, width = embeddings.shape
+    children, owned, _ = centroids.shape
     block = 2 * SHORT * DENSE_PAIRS
+    steps = devices // (2 * DENSE_PAIRS)
+    few = children // steps
+    finished = pl.BlockSpec((OWN, few, width), lambda i, *_: (0, i, 0))
     return pl.pallas_call(
         functools.partial(dense_pack_kernel, outers, owned),
-        out_shape=jax.ShapeDtypeStruct((devices * SHORT, width), jnp.bfloat16),
+        out_shape=(
+            pltpu.HBM((devices * SHORT, width), jnp.bfloat16),
+            jax.ShapeDtypeStruct((OWN, children, width), jnp.bfloat16),
+            jax.ShapeDtypeStruct((OWN, children, width), jnp.float32),
+        ),
         grid_spec=pltpu.PrefetchScalarGridSpec(
             num_scalar_prefetch=len(scalars),
-            grid=(devices // (2 * DENSE_PAIRS),),
+            grid=(steps,),
             in_specs=[
                 pl.BlockSpec((total, width), lambda i, *_: (0, 0), pipeline_mode=pl.Buffered(1)),
                 pl.BlockSpec((2, LANES), lambda i, *_: (0, 0), pipeline_mode=pl.Buffered(1)),
+                pl.BlockSpec((few, 8, width), lambda i, *p: (i, p[-1][0] >> 1, 0)),
             ],
-            out_specs=pl.BlockSpec((block, width), lambda i, *_: (i, 0)),
-            scratch_shapes=[pltpu.VMEM((total + WIN, width), jnp.bfloat16)],
+            out_specs=(pl.BlockSpec((block, width), lambda i, *_: (i, 0)), finished, finished),
+            scratch_shapes=[pltpu.VMEM((width // LANES, few * 8, LANES), jnp.float32)],
         ),
-        compiler_params=pltpu.CompilerParams(vmem_limit_bytes=54 << 20),
+        compiler_params=pltpu.CompilerParams(vmem_limit_bytes=62 << 20),
         name="dense_pack",
-    )(*scalars, embeddings, common)
+    )(*scalars, embeddings, common, centroids)
 
 
 def collect_kernel(me_ref, rows_ref, head_ref, late_ref, notes_ref, unfit_ref, wide_ref):
@@ -387,19 +416,28 @@
     )(me, arrived, arrived)
 
 
-def weighted_rows(low, rows, slots, shrink):
+def weighted_rows(low, rows, slots, shrink, piece):
     children = low.shape[0] // OWN
-    logits = lax.dot_general(
-        low, rows, (((1,), (1,)), ((), ())), preferred_element_type=jnp.float32
-    )
-    chosen = jnp.zeros((children, rows.shape[0]), jnp.float32)
-    for j in range(OWN):
-        chosen = jnp.where(slots == j, logits[j * children : (j + 1) * children], chosen)
-    raised = jnp.exp(chosen * shrink)
-    weights = raised / jnp.sum(raised, axis=0, keepdims=True)
-    spread = jnp.concatenate(
-        [jnp.where(slots == j, weights, 0.0) for j in range(OWN)], axis=0
-    ).astype(jnp.bfloat16)
+    spread = []
+    for at in range(0, rows.shape[0], piece):
+        here = slots[:, at : at + piece]
+        logits = lax.dot_general(
+            low,
+            rows[at : at + piece],
+            (((1,), (1,)), ((), ())),
+            preferred_element_type=jnp.float32,
+        )
+        chosen = jnp.zeros((children, piece), jnp.float32)
+        for j in range(OWN):
+            chosen = jnp.where(here == j, logits[j * children : (j + 1) * children], chosen)
+        raised = jnp.exp(chosen * shrink)
+        weights = raised / jnp.sum(raised, axis=0, keepdims=True)
+        spread.append(
+            jnp.concatenate(
+                [jnp.where(here == j, weights, 0.0) for j in range(OWN)], axis=0
+            ).astype(jnp.bfloat16)
+        )
+    spread = jnp.concatenate(spread, axis=1)
     return jnp.dot(spread, rows, preferred_element_type=jnp.float32)
 
 
@@ -413,7 +451,7 @@
 
 
 def dense_sums_kernel(shrink, rows_ref, notes_ref, low_ref, total_ref):
-    sums = weighted_rows(low_ref[...], rows_ref[...], along_lanes(notes_ref[...]), shrink)
+    sums = weighted_rows(low_ref[...], rows_ref[...], along_lanes(notes_ref[...]), shrink, 256)
 
     @pl.when(pl.program_id(0) == 0)
     def _():
@@ -426,7 +464,7 @@
 
 def dense_sums(arrived, notes, low, shrink):
     total, width = arrived.shape
-    block = 32 * SHORT
+    block = 64 * SHORT
     return pl.pallas_call(
         functools.partial(dense_sums_kernel, shrink),
         out_shape=jax.ShapeDtypeStruct(low.shape, jnp.float32),
@@ -458,7 +496,7 @@
         axis=0,
     )
     slots = along_lanes(notes) - 1 - OWN * node_ref[0]
-    added = weighted_rows(low_ref[...], late_ref[...], slots, shrink)
+    added = weighted_rows(low_ref[...], late_ref[...], slots, shrink, 256)
     parents = []
     for j in range(OWN):
         at = slice(j * children, (j + 1) * children)
@@ -487,48 +525,86 @@
     )(node, total, late, low, unit)
 
 
-def plan_kernel(outers, nodes, rank_ref, slot_ref, ids_ref, plan_ref, spill_ref, common_ref):
+def plan_kernel(
+    outers,
+    nodes,
+    rank_ref,
+    slot_ref,
+    ids_ref,
+    start_ref,
+    count_ref,
+    guests_ref,
+    turn_ref,
+    hosts_ref,
+    spill_ref,
+    common_ref,
+):
     slots = slot_ref.shape[1]
     owned = slots // outers
+    blocks = ids_ref.shape[0]
     room = SHORT - 1
-    row = lax.broadcasted_iota(jnp.int32, (slots, 1), 0)
-    other = lax.broadcasted_iota(jnp.int32, (1, slots), 1)
-    lane = lax.broadcasted_iota(jnp.int32, (1, LANES), 1)
-    parent = jnp.sum(
-        jnp.where(slot_ref[...] == row, other.astype(jnp.float32), 0.0), axis=1, keepdims=True
-    ).astype(jnp.int32)
-    ids = ids_ref[...]
-    starts = []
-    counts = []
-    for at in range(0, slots, 64):
-        mine = parent[at : at + 64]
-        below = jnp.where(ids < mine, 1.0, 0.0)
-        equal = jnp.where(ids == mine, 1.0, 0.0)
-        starts.append(jnp.sum(below, axis=1, keepdims=True))
-        counts.append(jnp.sum(equal, axis=1, keepdims=True))
-    starts = jnp.concatenate(starts, axis=0)
-    counts = jnp.concatenate(counts, axis=0)
-
-    def total(mask, columns):
-        wide = jnp.zeros((slots, LANES), jnp.float32)
-        for q, value in enumerate(columns):
-            wide = jnp.where(lane == q, value, wide)
-        mask = mask.astype(jnp.float32).astype(jnp.bfloat16)
-        sums = jnp.dot(mask, wide.astype(jnp.bfloat16), preferred_element_type=jnp.float32)
-        return [sums[:, q : q + 1] for q in range(len(columns))]
-
-    group = lax.shift_right_logical(row, 2)
-    other_group = lax.shift_right_logical(other, 2)
-    outer = lax.div(row, owned)
-    other_outer = lax.div(other, owned)
-    (first,) = total((group == other_group) & (other < row), [counts])
-    (sent,) = total(group == other_group, [counts])
+    wide = (slots, LANES)
+    row = lax.broadcasted_iota(jnp.int32, wide, 0)
+    lane = lax.broadcasted_iota(jnp.int32, wide, 1)
+    rows = row.astype(jnp.float32)
+    ones = jnp.ones((LANES, LANES), jnp.bfloat16)
+
+    def flag(mask):
+        return jnp.where(mask, 1.0, 0.0).astype(jnp.bfloat16)
+
+    def times(left, right):
+        return jnp.dot(left, right.astype(jnp.bfloat16), preferred_element_type=jnp.float32)
+
+    ids = jnp.concatenate(
+        [
+            ids_ref[...].astype(jnp.float32),
+            jnp.full((LANES - blocks, LANES), slots, jnp.float32),
+        ],
+        axis=0,
+    )
+    last = jnp.broadcast_to(jnp.transpose(ids)[LANES - 1 :, :], (8, LANES))
+    previous = pltpu.roll(last, 1, 1)[0:1]
+    last = last[0:1]
+    full = last < rows
+    reached = (lane == 0) | (previous < rows)
+    block = flag(reached & (last >= rows))
+    upper = jnp.floor(ids * 0.5)
+    inside = times(block, jnp.concatenate([upper, ids - 2.0 * upper], axis=1))
+    inside = 2.0 * inside[:, :LANES] + inside[:, LANES:]
+    begins = LANES * times(flag(full), ones) + times(flag(inside < rows), ones)
+    ends = pltpu.roll(begins, slots - 1, 0)
+    ends = jnp.where(row == slots - 1, float(blocks * LANES), ends)
+
+    other = lax.broadcasted_iota(jnp.int32, (slots, slots), 0)
+    mover = flag(slot_ref[...] == other)
+    upper = jnp.floor(begins * (1.0 / TILE))
+    moved = times(mover, jnp.concatenate([upper, begins - TILE * upper], axis=1))
+    starts = TILE * moved[:, :LANES] + moved[:, LANES:]
+    counts = times(mover, ends - begins)
+
+    def within(mask, *values):
+        parts = range(0, slots, LANES)
+        side = [value[at : at + LANES] for value in values for at in parts]
+        sums = times(flag(mask), jnp.concatenate(side, axis=1))
+        sums = [sums[:, at : at + LANES] for at in range(0, sums.shape[1], LANES)]
+        each = len(parts)
+        return [
+            jnp.concatenate(sums[v * each : (v + 1) * each], axis=0) for v in range(len(values))
+        ]
+
+    one = lax.broadcasted_iota(jnp.int32, (LANES, LANES), 0)
+    two = lax.broadcasted_iota(jnp.int32, (LANES, LANES), 1)
+    group_one, group_two = lax.shift_right_logical(one, 2), lax.shift_right_logical(two, 2)
+    same_group = group_one == group_two
+    same_outer = lax.div(one, owned) == lax.div(two, owned)
+    (first,) = within(same_group & (two < one), counts)
+    (sent,) = within(same_group, counts)
     over = jnp.maximum(sent - room, 0.0)
     host = jnp.where(sent <= room - GUESTS, 1.0, 0.0)
     once = jnp.where((row & (OWN - 1)) == 0, 1.0, 0.0)
-    parts = [over * once, host * once]
-    over_first, host_first = total((outer == other_outer) & (other_group < group), parts)
-    overs, real_hosts = total(outer == other_outer, parts)
+    parts = (over * once, host * once)
+    over_first, host_first = within(same_outer & (group_two < group_one), *parts)
+    overs, real_hosts = within(same_outer, *parts)
     hosts = jnp.maximum(real_hosts, 1.0)
     shift = jnp.zeros_like(hosts)
     for h in range(1, nodes + 1):
@@ -540,10 +616,12 @@
     )
     failed = jnp.max(overs - GUESTS * real_hosts) > 0.0
 
-    wide = jnp.zeros((slots, LANES), jnp.float32)
+    flat = jnp.zeros(wide, jnp.float32)
     for q, value in enumerate([starts, counts, guests, turn, hosts]):
-        wide = jnp.where(lane == q, value, wide)
-    plan_ref[...] = jnp.transpose(wide)[:8].astype(jnp.int32)
+        flat = jnp.where(lane == q, value, flat)
+    flat = jnp.transpose(flat)[:8].astype(jnp.int32)
+    for q, ref in enumerate([start_ref, count_ref, guests_ref, turn_ref, hosts_ref]):
+        ref[...] = flat[q : q + 1].reshape(slots)
 
     begin = over_first + jnp.maximum(first - room, 0.0)
     end = over_first + jnp.maximum(first + counts - room, 0.0)
@@ -557,8 +635,8 @@
         spill_ref[outers + o : outers + o + 1, :] = jnp.sum(
             named[at], axis=0, keepdims=True
         ).astype(jnp.int32)
-    where = (lane & (outers - 1)) * owned + lax.div(lane, outers) * OWN
-    common_ref[0:1, :] = jnp.sum(jnp.where(row == where, guests, 0.0), axis=0, keepdims=True)
+    device = (lane & (outers - 1)) * owned + lax.div(lane, outers) * OWN
+    common_ref[0:1, :] = jnp.sum(jnp.where(row == device, guests, 0.0), axis=0, keepdims=True)
     common_ref[1:2, :] = jnp.broadcast_to(failed.astype(jnp.float32), (1, LANES))
 
 
@@ -567,14 +645,14 @@
     return pl.pallas_call(
         functools.partial(plan_kernel, outers, nodes),
         out_shape=(
-            jax.ShapeDtypeStruct((8, slots), jnp.int32),
-            jax.ShapeDtypeStruct((2 * outers, LANES), jnp.int32),
+            *[pltpu.HBM((slots,), jnp.int32)] * 5,
+            pltpu.HBM((2 * outers, LANES), jnp.int32),
             jax.ShapeDtypeStruct((2, LANES), jnp.float32),
         ),
         in_specs=[pl.BlockSpec(memory_space=pltpu.SMEM)]
         + [pl.BlockSpec(memory_space=pltpu.VMEM)] * 2,
         name="plan",
-    )(rank, parent_slot.reshape(1, -1), embedding_parent_index.reshape(1, -1))
+    )(rank, parent_slot.reshape(1, -1), embedding_parent_index.reshape(-1, LANES))
 
 
 def body(embeddings, embedding_parent_index, parent_slot, centroids):
@@ -588,22 +666,20 @@
     everyone = ("node", "outer")
     rank = lax.axis_index(everyone)
 
-    own = lax.dynamic_slice_in_dim(centroids, node * OWN, OWN, 1).transpose(1, 0, 2)
-    unit = unit_scale(own.astype(jnp.float32))
-    low = unit.astype(jnp.bfloat16)
-    places, spill, common = plan(
-        parent_slot, embedding_parent_index, rank.reshape(1), outers, nodes
+    me, here = rank.reshape(1), node.reshape(1)
+    *places, common = plan(parent_slot, embedding_parent_index, me, outers, nodes)
+    packed, low, unit = dense_pack(
+        embeddings, (*places, here), common, centroids, outers, devices
     )
-    packed = dense_pack(embeddings, (places, spill), common, outers, owned, devices)
-    packed, unit, low, embeddings, places, me, here = lax.optimization_barrier(
-        (packed, unit, low, embeddings, places, rank.reshape(1), node.reshape(1))
+    packed, unit, low, embeddings, starts, counts, me, here = lax.optimization_barrier(
+        (packed, unit, low, embeddings, *places[:2], me, here)
     )
     arrived = lax.all_to_all(
         packed.reshape(devices, SHORT, width), everyone, split_axis=0, concat_axis=0, tiled=True
     )
     late, notes, unfit = collect(arrived, me, nodes)
-    unfit, unit, low, embeddings, places, here = lax.optimization_barrier(
-        (unfit, unit, low, embeddings, places, here)
+    unfit, unit, low, embeddings, starts, counts, here = lax.optimization_barrier(
+        (unfit, unit, low, embeddings, starts, counts, here)
     )
 
     def short_way():
@@ -615,7 +691,7 @@
         )
 
     def long_way():
-        full = pack(embeddings, places[0], places[1], outers, owned, devices)
+        full = pack(embeddings, starts, counts, outers, owned, devices)
         full = lax.all_to_all(
             full.reshape(devices, ROWS, width), everyone, split_axis=0, concat_axis=0, tiled=True
         )

time: 187 us -> 179 us (0.957)
  Pallas kernels: 47.6 us -> 42.3 us
  local copies, waits for them, and re-layouts: 2.15 us -> 0.01 us
  other arithmetic: 2.12 us -> 0 us
    pallas_call x1, Pallas kernels: 19 us -> 15.5 us  [dense_pack(): pl.pallas_call(functools.partial(dense_pack_kernel, outers, owned), out_s...]
    dynamic_slice x1 -> x0, local copies, waits for them, and re-layouts: 2.14 us -> none  [body(): lax.dynamic_slice_in_dim(centroids, node * OWN, OWN, 1).transpose(1, 0, 2)]
where the time goes in v3:
time: 179 us
  blocking collectives  131 us (73%)
  Pallas kernels  42.3 us (24%)
  starting transfers between devices  4.13 us (2%)
    all_to_all x1, blocking collectives, body(): lax.all_to_all(packed.reshape(devices, SHORT, width), everyone, split_axi...  110 us
    all_to_all x1, blocking collectives, body(): lax.all_to_all(fresh, 'node', split_axis=0, concat_axis=0, tiled=True)  21.4 us
    pallas_call x1, Pallas kernels, dense_pack(): pl.pallas_call(functools.partial(dense_pack_kernel, outers, owned), out_s...  15.5 us
    pallas_call x1, Pallas kernels, dense_sums(): pl.pallas_call(functools.partial(dense_sums_kernel, shrink), out_shape=ja...  11.9 us
    pallas_call x1, Pallas kernels, finish(): pl.pallas_call(functools.partial(finish_kernel, shrink, per_node), out_sh...  4.83 us
    all_to_all x1, starting transfers between devices, short_way(): lax.all_to_all(late, 'node', split_axis=0, concat_axis=0, tiled=True)  4.13 us
    pallas_call x1, Pallas kernels, put_in_order(): pl.pallas_call(functools.partial(order_kernel, per_node), out_shape=(jax....  3.63 us
  transfers between devices with their start and end apart: 1, of which 0 were waited for; matrix products, arithmetic and copies ran while one was open for 0% of the time, Pallas kernels for 7%

profile of v3, /device:TPU:1, one launch (start us, length us, event | category | flops | bytes accessed | tf_op | source)
XLA Modules:
  0.0 179.2 jit_solution(737675077638028338)
XLA Ops:
  0.6 3.0 %plan.1 = (s32[512]{0:T(512)}, s32[512]{0:T(512)}, s32[512]{0:T(512)}, s32[512]{0:T(512)}, s32[512]{0:T(512)}, /*index=5*/s32[32,128]{1,0:T(8,128)}, f32[2,128]{1,0:T(2,128)}) custom-call(s32[1]{0:T(128)} %bitcast.5.rank_ref.me_ref, s32[1,512]{1,0:T(1,128)} %bitcast.22, s32[24,128]{1,0:T(8,128)} %bitcast.21), custom_call_target="tpu_custom_call" | custom-call | tf_op jit(solution)/shard_map/plan/pallas_call | solution.py:645
  3.6 15.5 %dense_pack.1 = (bf16[4096,1024]{1,0:T(8,128)(2,1)}, bf16[4,128,1024]{2,1,0:T(8,128)(2,1)S(1)}, f32[4,128,1024]{2,1,0:T(8,128)}) custom-call(s32[512]{0:T(512)} %get-tuple-element.93.start_ref, s32[512]{0:T(512)} %get-tuple-element.94.count_ref, s32[512]{0:T(512)} %get-tuple-element.70.guests_ref, s32[512]{0:T(512)} %get-tuple-element.71.turn_ref, ...), custom_call_target="tpu_custom_call" | custom-call | tf_op jit(solution)/shard_map/dense_pack/pallas_call | solution.py:326
  19.1 110.0 %all_to_all.19.rows_ref.head_ref = bf16[128,32,1024]{2,1,0:T(8,128)(2,1)} all-to-all(bf16[128,32,1024]{2,1,0:T(8,128)(2,1)} %bitcast.17), channel_id=1, replica_groups=mesh['node'=8,'outer'=16] {'node','outer'}, dimensions={0} | all-to-all | bytes 16777216 | tf_op jit(solution)/shard_map/all_to_all | solution.py:677
  129.1 0.0 copy-start.2
  129.1 0.0 copy-start.3
  129.1 3.4 %collect.1 = (bf16[8,32,1024]{2,1,0:T(8,128)(2,1)}, f32[128,128]{1,0:T(8,128)S(1)}, s32[1]{0:T(128)}) custom-call(s32[1]{0:T(128)} %bitcast.5.rank_ref.me_ref, bf16[128,32,1024]{2,1,0:T(8,128)(2,1)} %all_to_all.19.rows_ref.head_ref, bf16[128,32,1024]{2,1,0:T(8,128)(2,1)} %all_to_all.19.rows_ref.head_ref), custom_call_target="tpu_custom_call" | custom-call | tf_op jit(solution)/shard_map/collect/pallas_call | solution.py:393
  133.2 0.0 copy-done.2
  133.2 0.0 copy-done.3
  133.2 20.9 %conditional.1 = (bf16[8,72,1024]{2,1,0:T(8,128)(2,1)}) conditional(s32[]{:T(128)} %bitcast.10, (bf16[128,32,1024]{2,1,0:T(8,128)(2,1)}, bf16[4,128,1024]{2,1,0:T(8,128)(2,1)S(1)}, f32[128,128]{1,0:T(8,128)S(1)}, bf16[8,32,1024]{2,1,0:T(8,128)(2,1)}, s32[1]{0:T(128)}, /*index=5*/f32[4,128,1024]{2,1,0:T(8,128)}) %tuple.18, (s32[512]{0:T(512)S(1)}, ...), branch_computations={%region_0.0_spmd, %region_1.0_spmd} | conditional | flops 8589934592 | bytes 33554468 | solution.py:700
  133.2 0.0 copy-start.1
  133.2 4.1 %all-to-all-start = ((bf16[8,32,1024]{2,1,0:T(8,128)(2,1)}), bf16[8,32,1024]{2,1,0:T(8,128)(2,1)S(1)}, u32[]{:S(2)}, u32[]{:S(2)}) async-start(bf16[8,32,1024]{2,1,0:T(8,128)(2,1)} %get-tuple-element.29), calls=%async_computation | async-start | bytes 1048576 | tf_op jit(solution)/shard_map/cond/branch_0_fun/all_to_all | solution.py:686
  137.3 0.0 copy-done.1
  137.3 11.9 %dense_sums.1.total_ref = f32[512,1024]{1,0:T(8,128)S(1)} custom-call(bf16[4096,1024]{1,0:T(8,128)(2,1)} %bitcast.15, f32[128,128]{1,0:T(8,128)S(1)} %get-tuple-element.27.notes_ref, bf16[512,1024]{1,0:T(8,128)(2,1)} %bitcast.19), custom_call_target="tpu_custom_call" | custom-call | flops 8589934592 | bytes 11534336 | tf_op jit(solution)/shard_map/cond/branch_0_fun/dense_sums/pallas_call | solution.py:468
  149.3 0.0 all-to-all-done
  149.3 4.8 %finish.1 = bf16[8,72,1024]{2,1,0:T(8,128)(2,1)} custom-call(s32[1]{0:T(128)} %get-tuple-element.16.node_ref, f32[512,1024]{1,0:T(8,128)S(1)} %dense_sums.1.total_ref, bf16[256,1024]{1,0:T(8,128)(2,1)S(1)} %bitcast.14, bf16[512,1024]{1,0:T(8,128)(2,1)} %bitcast.20, f32[4,128,1024]{2,1,0:T(8,128)} %get-tuple-element.30.unit_ref), custom_call_target="tpu_custom_call" | custom-call | tf_op jit(solution)/shard_map/cond/branch_0_fun/finish/pallas_call | solution.py:518
  154.1 21.4 %all_to_all.20 = bf16[8,72,1024]{2,1,0:T(8,128)(2,1)} all-to-all(bf16[8,72,1024]{2,1,0:T(8,128)(2,1)} %get-tuple-element.98), channel_id=1, replica_groups=mesh['node'=8,'outer'=16] {'node'}, dimensions={0} | all-to-all | bytes 2359296 | tf_op jit(solution)/shard_map/all_to_all | solution.py:701
  175.6 3.6 %put_in_order.1 = (f32[512,1024]{1,0:T(8,128)}, f32[32,1024]{1,0:T(8,128)}) custom-call(bf16[576,1024]{1,0:T(8,128)(2,1)} %bitcast.18), custom_call_target="tpu_custom_call" | custom-call | tf_op jit(solution)/shard_map/put_in_order/pallas_call | solution.py:186
Async XLA Ops:
  129.1 4.1 %copy-start.2 = (s32[512]{0:T(512)S(1)}, s32[512]{0:T(512)}, u32[]{:S(2)}) copy-start(s32[512]{0:T(512)} %get-tuple-element.93.start_ref) | copy-start | bytes 6148
  129.1 4.1 %copy-start.3 = (s32[512]{0:T(512)S(1)}, s32[512]{0:T(512)}, u32[]{:S(2)}) copy-start(s32[512]{0:T(512)} %get-tuple-element.94.count_ref) | copy-start | bytes 6148
  133.2 4.1 %copy-start.1 = (bf16[4,128,1024]{2,1,0:T(8,128)(2,1)}, bf16[4,128,1024]{2,1,0:T(8,128)(2,1)S(1)}, u32[]{:S(2)}) copy-start(bf16[4,128,1024]{2,1,0:T(8,128)(2,1)S(1)} %get-tuple-element.28) | copy-start | bytes 3145732 | tf_op jit(solution)/shard_map/cond
  133.2 16.1 %all-to-all-start = ((bf16[8,32,1024]{2,1,0:T(8,128)(2,1)}), bf16[8,32,1024]{2,1,0:T(8,128)(2,1)S(1)}, u32[]{:S(2)}, u32[]{:S(2)}) async-start(bf16[8,32,1024]{2,1,0:T(8,128)(2,1)} %get-tuple-element.29), calls=%async_computation | async-start | bytes 1048576 | tf_op jit(solution)/shard_map/cond/branch_0_fun/all_to_all | solution.py:686

commit v4 on v3

--- a/solution.py
+++ b/solution.py
@@ -197,23 +197,32 @@
 def dense_pack_kernel(
     outers,
     owned,
-    start_ref,
-    count_ref,
-    guests_ref,
-    turn_ref,
-    hosts_ref,
-    spill_ref,
+    nodes,
+    me_ref,
     node_ref,
-    rows_ref,
-    common_ref,
+    slot_ref,
+    ids_ref,
+    far_rows_ref,
     centroid_ref,
     out_ref,
     low_ref,
     unit_ref,
+    rows_ref,
     wide_ref,
+    common_ref,
+    *work,
 ):
+    planned, placed, done = work[:6], work[6:12], work[12]
+    start_ref, count_ref, guests_ref, turn_ref, hosts_ref, spill_ref = placed
     total, width = rows_ref.shape
     step = pl.program_id(0)
+
+    @pl.when(step == 0)
+    def _():
+        fetch = pltpu.make_async_copy(far_rows_ref, rows_ref, done.at[len(placed)])
+        fetch.start()
+        plan_kernel(outers, nodes, me_ref, slot_ref, ids_ref, *planned, common_ref)
+
     outer_bits = outers.bit_length() - 1
     centroids = centroid_ref[...].astype(jnp.float32).reshape(wide_ref.shape[1], width)
     for c in range(width // LANES):
@@ -225,6 +234,17 @@
         unit = unit_scale(jnp.concatenate(mine, axis=1))
         unit_ref[j] = unit
         low_ref[j] = unit.astype(jnp.bfloat16)
+
+    @pl.when(step == 0)
+    def _():
+        copies = [
+            pltpu.make_async_copy(planned[i], placed[i], done.at[i]) for i in range(len(placed))
+        ]
+        for copy in copies:
+            copy.start()
+        for copy in copies:
+            copy.wait()
+        pltpu.make_async_copy(far_rows_ref, rows_ref, done.at[len(placed)]).wait()
 
     place = lax.broadcasted_iota(jnp.int32, (SHORT, 1), 0) - 1
     column = lax.broadcasted_iota(jnp.int32, (SHORT, 2 * OWN * WIN), 1)
@@ -277,73 +297,85 @@
         device = step * 2 * DENSE_PAIRS + m
         return (device & (outers - 1)) * owned + (device >> outer_bits) * OWN
 
-    def seat(m, carry):
-        base = base_of(m)
-        outer = lax.div(base, owned)
-        for i in range(GUESTS):
-
-            @pl.when(guests_ref[base] > i)
-            def _():
-                entry = turn_ref[base] + i * hosts_ref[base]
-                source = spill_ref[outer, entry]
-                slot = spill_ref[outers + outer, entry].astype(jnp.float32)
-                aligned = lax.shift_left(lax.shift_right_logical(source, 4), 4)
-                tile = rows_ref[pl.ds(pl.multiple_of(aligned, TILE), TILE), :].astype(jnp.float32)
-                chosen = unit_scale(
-                    jnp.sum(
-                        jnp.where(tile_row == source - aligned, tile, 0.0), axis=0, keepdims=True
-                    )
-                )
-                tail = pl.ds(pl.multiple_of(m * SHORT + TILE, TILE), TILE)
-                kept = out_ref[tail, :].astype(jnp.float32)
-                out_ref[tail, :] = jnp.where(tile_row == TILE - 1 - i, chosen, kept).astype(
-                    jnp.bfloat16
-                )
-                head = pl.ds(pl.multiple_of(m * SHORT, TILE), TILE)
-                where = slice(3 * LANES, 4 * LANES)
-                kept = out_ref[head, where].astype(jnp.float32)
-                mine = (tile_row == 0) & ((lane & 7) == 7 - i)
-                out_ref[head, where] = jnp.where(mine, slot, kept).astype(jnp.bfloat16)
-
-        return carry
-
-    seated = guests_ref[base_of(0)]
-    for m in range(1, 2 * DENSE_PAIRS):
-        seated = seated + guests_ref[base_of(m)]
+    def seat(m, base, i):
+        outer = lax.shift_right_logical(base, owned.bit_length() - 1)
+        entry = turn_ref[base] + i * hosts_ref[base]
+        source = spill_ref[outer, entry]
+        slot = spill_ref[outers + outer, entry].astype(jnp.float32)
+        aligned = lax.shift_left(lax.shift_right_logical(source, 4), 4)
+        tile = rows_ref[pl.ds(pl.multiple_of(aligned, TILE), TILE), :].astype(jnp.float32)
+        chosen = unit_scale(
+            jnp.sum(jnp.where(tile_row == source - aligned, tile, 0.0), axis=0, keepdims=True)
+        )
+        tail = slice(m * SHORT + TILE, (m + 1) * SHORT)
+        kept = out_ref[tail, :].astype(jnp.float32)
+        out_ref[tail, :] = jnp.where(tile_row == TILE - 1 - i, chosen, kept).astype(jnp.bfloat16)
+        head = slice(m * SHORT, m * SHORT + TILE)
+        where = slice(3 * LANES, 4 * LANES)
+        kept = out_ref[head, where].astype(jnp.float32)
+        mine = (tile_row == 0) & ((lane & 7) == 7 - i)
+        out_ref[head, where] = jnp.where(mine, slot, kept).astype(jnp.bfloat16)
+
+    bases = [base_of(m) for m in range(2 * DENSE_PAIRS)]
+    seated = guests_ref[bases[0]]
+    for base in bases[1:]:
+        seated = seated + guests_ref[base]
 
     @pl.when(seated > 0)
     def _():
-        lax.fori_loop(0, 2 * DENSE_PAIRS, seat, 0)
-
-
-def dense_pack(embeddings, scalars, common, centroids, outers, devices):
+        for m, base in enumerate(bases):
+            guests = guests_ref[base]
+
+            @pl.when(guests > 0)
+            def _():
+                seat(m, base, 0)
+
+                @pl.when(guests > 1)
+                def _():
+                    seat(m, base, 1)
+
+
+def dense_pack(embeddings, parent_slot, ids, centroids, me, node, outers, nodes):
     total, width = embeddings.shape
     children, owned, _ = centroids.shape
+    slots = parent_slot.shape[0]
+    devices = outers * nodes
     block = 2 * SHORT * DENSE_PAIRS
     steps = devices // (2 * DENSE_PAIRS)
     few = children // steps
     finished = pl.BlockSpec((OWN, few, width), lambda i, *_: (0, i, 0))
+    shapes = [(slots,)] * 5 + [(2 * outers, LANES)]
     return pl.pallas_call(
-        functools.partial(dense_pack_kernel, outers, owned),
+        functools.partial(dense_pack_kernel, outers, owned, nodes),
         out_shape=(
             pltpu.HBM((devices * SHORT, width), jnp.bfloat16),
             jax.ShapeDtypeStruct((OWN, children, width), jnp.bfloat16),
             jax.ShapeDtypeStruct((OWN, children, width), jnp.float32),
         ),
         grid_spec=pltpu.PrefetchScalarGridSpec(
-            num_scalar_prefetch=len(scalars),
+            num_scalar_prefetch=2,
             grid=(steps,),
             in_specs=[
-                pl.BlockSpec((total, width), lambda i, *_: (0, 0), pipeline_mode=pl.Buffered(1)),
-                pl.BlockSpec((2, LANES), lambda i, *_: (0, 0), pipeline_mode=pl.Buffered(1)),
-                pl.BlockSpec((few, 8, width), lambda i, *p: (i, p[-1][0] >> 1, 0)),
+                pl.BlockSpec((1, slots), lambda i, *_: (0, 0), pipeline_mode=pl.Buffered(1)),
+                pl.BlockSpec(
+                    (total // LANES, LANES), lambda i, *_: (0, 0), pipeline_mode=pl.Buffered(1)
+                ),
+                pl.BlockSpec(memory_space=pltpu.HBM),
+                pl.BlockSpec((few, 8, width), lambda i, m, n: (i, n[0] >> 1, 0)),
             ],
             out_specs=(pl.BlockSpec((block, width), lambda i, *_: (i, 0)), finished, finished),
-            scratch_shapes=[pltpu.VMEM((width // LANES, few * 8, LANES), jnp.float32)],
+            scratch_shapes=[
+                pltpu.VMEM((total, width), jnp.bfloat16),
+                pltpu.VMEM((width // LANES, few * 8, LANES), jnp.float32),
+                pltpu.VMEM((2, LANES), jnp.float32),
+                *[pltpu.VMEM(shape, jnp.int32) for shape in shapes],
+                *[pltpu.SMEM(shape, jnp.int32) for shape in shapes],
+                pltpu.SemaphoreType.DMA((len(shapes) + 1,)),
+            ],
         ),
         compiler_params=pltpu.CompilerParams(vmem_limit_bytes=62 << 20),
         name="dense_pack",
-    )(*scalars, embeddings, common, centroids)
+    )(me, node, parent_slot.reshape(1, -1), ids.reshape(-1, LANES), embeddings, centroids)
 
 
 def collect_kernel(me_ref, rows_ref, head_ref, late_ref, notes_ref, unfit_ref, wide_ref):
@@ -667,19 +699,19 @@
     rank = lax.axis_index(everyone)
 
     me, here = rank.reshape(1), node.reshape(1)
-    *places, common = plan(parent_slot, embedding_parent_index, me, outers, nodes)
     packed, low, unit = dense_pack(
-        embeddings, (*places, here), common, centroids, outers, devices
+        embeddings, parent_slot, embedding_parent_index, centroids, me, here, outers, nodes
     )
-    packed, unit, low, embeddings, starts, counts, me, here = lax.optimization_barrier(
-        (packed, unit, low, embeddings, *places[:2], me, here)
+    given = (embeddings, parent_slot, embedding_parent_index)
+    packed, unit, low, me, here, *given = lax.optimization_barrier(
+        (packed, unit, low, me, here, *given)
     )
     arrived = lax.all_to_all(
         packed.reshape(devices, SHORT, width), everyone, split_axis=0, concat_axis=0, tiled=True
     )
     late, notes, unfit = collect(arrived, me, nodes)
-    unfit, unit, low, embeddings, starts, counts, here = lax.optimization_barrier(
-        (unfit, unit, low, embeddings, starts, counts, here)
+    unfit, unit, low, me, here, *given = lax.optimization_barrier(
+        (unfit, unit, low, me, here, *given)
     )
 
     def short_way():
@@ -691,7 +723,8 @@
         )
 
     def long_way():
-        full = pack(embeddings, starts, counts, outers, owned, devices)
+        starts, counts, *_ = plan(given[1], given[2], me, outers, nodes)
+        full = pack(given[0], starts, counts, outers, owned, devices)
         full = lax.all_to_all(
             full.reshape(devices, ROWS, width), everyone, split_axis=0, concat_axis=0, tiled=True
         )

time: 179 us -> 175 us (0.978)
  Pallas kernels: 42.3 us -> 38.6 us
    pallas_call x2 -> x1, Pallas kernels: 18.5 us -> 14.8 us  [dense_pack(): pl.pallas_call(functools.partial(dense_pack_kernel, outers, owned, nodes)...]
where the time goes in v4:
time: 175 us; the launch traced here: 174 us
  blocking collectives  130 us (74%)
  Pallas kernels  38.6 us (22%)
  starting transfers between devices  4.13 us (2%)
    all_to_all x1, blocking collectives, body(): lax.all_to_all(packed.reshape(devices, SHORT, width), everyone, split_axi...  109 us
    all_to_all x1, blocking collectives, body(): lax.all_to_all(fresh, 'node', split_axis=0, concat_axis=0, tiled=True)  21.4 us
    pallas_call x1, Pallas kernels, dense_pack(): pl.pallas_call(functools.partial(dense_pack_kernel, outers, owned, nodes)...  14.8 us
    pallas_call x1, Pallas kernels, dense_sums(): pl.pallas_call(functools.partial(dense_sums_kernel, shrink), out_shape=ja...  11.9 us
    pallas_call x1, Pallas kernels, finish(): pl.pallas_call(functools.partial(finish_kernel, shrink, per_node), out_sh...  4.84 us
    all_to_all x1, starting transfers between devices, short_way(): lax.all_to_all(late, 'node', split_axis=0, concat_axis=0, tiled=True)  4.13 us
    pallas_call x1, Pallas kernels, put_in_order(): pl.pallas_call(functools.partial(order_kernel, per_node), out_shape=(jax....  3.63 us
  transfers between devices with their start and end apart: 1, of which 0 were waited for; matrix products, arithmetic and copies ran while one was open for 0% of the time, Pallas kernels for 7%

profile of v4, /device:TPU:1, one launch (start us, length us, event | category | flops | bytes accessed | tf_op | source)
XLA Modules:
  0.0 174.1 jit_solution(13356900002884341913)
XLA Ops:
  0.6 14.8 %dense_pack.1 = (bf16[4096,1024]{1,0:T(8,128)(2,1)}, bf16[4,128,1024]{2,1,0:T(8,128)(2,1)S(1)}, f32[4,128,1024]{2,1,0:T(8,128)}) custom-call(s32[1]{0:T(128)} %bitcast.7.me_ref, s32[1]{0:T(128)} %bitcast.8.node_ref, s32[1,512]{1,0:T(1,128)} %bitcast.25, s32[24,128]{1,0:T(8,128)} %bitcast.23, bf16[3072,1024]{1,0:T(8,128)(2,1)} %far_rows_ref.1, ...), custom_call_target="tpu_custom_call" | custom-call | tf_op jit(solution)/shard_map/dense_pack/pallas_call | solution.py:348
  15.4 108.6 %all_to_all.19.rows_ref.head_ref = bf16[128,32,1024]{2,1,0:T(8,128)(2,1)} all-to-all(bf16[128,32,1024]{2,1,0:T(8,128)(2,1)} %bitcast.19), channel_id=1, replica_groups=mesh['node'=8,'outer'=16] {'node','outer'}, dimensions={0} | all-to-all | bytes 16777216 | tf_op jit(solution)/shard_map/all_to_all | solution.py:709
  124.0 0.0 copy-start.4
  124.0 0.0 copy-start.5
  124.0 3.4 %collect.1 = (bf16[8,32,1024]{2,1,0:T(8,128)(2,1)}, f32[128,128]{1,0:T(8,128)S(1)}, s32[1]{0:T(128)}) custom-call(s32[1]{0:T(128)} %bitcast.7.me_ref, bf16[128,32,1024]{2,1,0:T(8,128)(2,1)} %all_to_all.19.rows_ref.head_ref, bf16[128,32,1024]{2,1,0:T(8,128)(2,1)} %all_to_all.19.rows_ref.head_ref), custom_call_target="tpu_custom_call" | custom-call | tf_op jit(solution)/shard_map/collect/pallas_call | solution.py:425
  128.0 0.0 copy-done.4
  128.1 0.0 copy-done.5
  128.1 21.0 %conditional.1 = (bf16[8,72,1024]{2,1,0:T(8,128)(2,1)}) conditional(s32[]{:T(128)} %bitcast.12, (bf16[128,32,1024]{2,1,0:T(8,128)(2,1)}, bf16[4,128,1024]{2,1,0:T(8,128)(2,1)S(1)}, f32[128,128]{1,0:T(8,128)S(1)}, bf16[8,32,1024]{2,1,0:T(8,128)(2,1)}, s32[1]{0:T(128)}, /*index=5*/f32[4,128,1024]{2,1,0:T(8,128)}) %tuple.18, (s32[512]{0:T(512)S(1)}, ...), branch_computations={%region_0.0_spmd, %region_1.0_spmd} | conditional | flops 8589934592 | bytes 33570908 | solution.py:733
  128.1 0.0 copy-start.3
  128.1 4.1 %all-to-all-start = ((bf16[8,32,1024]{2,1,0:T(8,128)(2,1)}), bf16[8,32,1024]{2,1,0:T(8,128)(2,1)S(1)}, u32[]{:S(2)}, u32[]{:S(2)}) async-start(bf16[8,32,1024]{2,1,0:T(8,128)(2,1)} %get-tuple-element.31), calls=%async_computation | async-start | bytes 1048576 | tf_op jit(solution)/shard_map/cond/branch_0_fun/all_to_all | solution.py:718
  132.2 0.0 copy-done.3
  132.2 11.9 %dense_sums.1.total_ref = f32[512,1024]{1,0:T(8,128)S(1)} custom-call(bf16[4096,1024]{1,0:T(8,128)(2,1)} %bitcast.17, f32[128,128]{1,0:T(8,128)S(1)} %get-tuple-element.29.notes_ref, bf16[512,1024]{1,0:T(8,128)(2,1)} %bitcast.21), custom_call_target="tpu_custom_call" | custom-call | flops 8589934592 | bytes 11534336 | tf_op jit(solution)/shard_map/cond/branch_0_fun/dense_sums/pallas_call | solution.py:500
  144.2 0.0 all-to-all-done
  144.2 4.8 %finish.1 = bf16[8,72,1024]{2,1,0:T(8,128)(2,1)} custom-call(s32[1]{0:T(128)} %get-tuple-element.17.node_ref, f32[512,1024]{1,0:T(8,128)S(1)} %dense_sums.1.total_ref, bf16[256,1024]{1,0:T(8,128)(2,1)S(1)} %bitcast.16, bf16[512,1024]{1,0:T(8,128)(2,1)} %bitcast.22, f32[4,128,1024]{2,1,0:T(8,128)} %get-tuple-element.32.unit_ref), custom_call_target="tpu_custom_call" | custom-call | tf_op jit(solution)/shard_map/cond/branch_0_fun/finish/pallas_call | solution.py:550
  149.0 21.4 %all_to_all.20 = bf16[8,72,1024]{2,1,0:T(8,128)(2,1)} all-to-all(bf16[8,72,1024]{2,1,0:T(8,128)(2,1)} %get-tuple-element.91), channel_id=1, replica_groups=mesh['node'=8,'outer'=16] {'node'}, dimensions={0} | all-to-all | bytes 2359296 | tf_op jit(solution)/shard_map/all_to_all | solution.py:734
  170.4 3.6 %put_in_order.1 = (f32[512,1024]{1,0:T(8,128)}, f32[32,1024]{1,0:T(8,128)}) custom-call(bf16[576,1024]{1,0:T(8,128)(2,1)} %bitcast.20), custom_call_target="tpu_custom_call" | custom-call | tf_op jit(solution)/shard_map/put_in_order/pallas_call | solution.py:186
Async XLA Ops:
  124.0 4.1 %copy-start.4 = (s32[3072]{0:T(1024)S(1)}, s32[3072]{0:T(1024)}, u32[]{:S(2)}) copy-start(s32[3072]{0:T(1024)} %param.7) | copy-start | bytes 36868
  124.0 4.1 %copy-start.5 = (s32[512]{0:T(512)S(1)}, s32[512]{0:T(512)}, u32[]{:S(2)}) copy-start(s32[512]{0:T(512)} %param.8) | copy-start | bytes 6148
  128.1 4.1 %copy-start.3 = (bf16[4,128,1024]{2,1,0:T(8,128)(2,1)}, bf16[4,128,1024]{2,1,0:T(8,128)(2,1)S(1)}, u32[]{:S(2)}) copy-start(bf16[4,128,1024]{2,1,0:T(8,128)(2,1)S(1)} %get-tuple-element.30) | copy-start | bytes 3145732 | tf_op jit(solution)/shard_map/cond
  128.1 16.1 %all-to-all-start = ((bf16[8,32,1024]{2,1,0:T(8,128)(2,1)}), bf16[8,32,1024]{2,1,0:T(8,128)(2,1)S(1)}, u32[]{:S(2)}, u32[]{:S(2)}) async-start(bf16[8,32,1024]{2,1,0:T(8,128)(2,1)} %get-tuple-element.31), calls=%async_computation | async-start | bytes 1048576 | tf_op jit(solution)/shard_map/cond/branch_0_fun/all_to_all | solution.py:718

commit v5 on v4

--- a/solution.py
+++ b/solution.py
@@ -268,10 +268,18 @@
                 aligned = lax.shift_left(lax.shift_right_logical(start, 4), 4)
                 aligned = jnp.minimum(aligned, total - WIN)
                 windows.append(rows_ref[pl.ds(pl.multiple_of(aligned, TILE), WIN), :])
+                count = count_ref[base + j]
+                if j == OWN - 1:
+                    target = jnp.where(place < at, target, -1)
+                    slots = jnp.where(lane_place < at, slots, NOBODY)
+                    sent = jnp.minimum(at + count, SHORT - 1)
+                    last = jnp.where(sent > SHORT - 1 - GUESTS, SHORT - 1, SHORT - 1 - GUESTS)
+                    at = at + last - sent
                 spot = (h * OWN + j) * WIN + (start - aligned) - at
                 target = jnp.where(place >= at, place + spot, target)
                 slots = jnp.where(lane_place >= at, j, slots)
-                at = at + count_ref[base + j]
+                at = at + count
+            at = jnp.minimum(at, last)
             target = jnp.where(place < at, target, -1)
             slots = jnp.where(lane_place < at, slots, NOBODY)
             selectors.append(jnp.where(column == target, 1.0, 0.0).astype(jnp.bfloat16))
@@ -448,8 +456,8 @@
     )(me, arrived, arrived)
 
 
-def weighted_rows(low, rows, slots, shrink, piece):
-    children = low.shape[0] // OWN
+def weighted_rows(low, rows, slots, shrink, piece, owners=OWN):
+    children = low.shape[0] // owners
     spread = []
     for at in range(0, rows.shape[0], piece):
         here = slots[:, at : at + piece]
@@ -460,13 +468,13 @@
             preferred_element_type=jnp.float32,
         )
         chosen = jnp.zeros((children, piece), jnp.float32)
-        for j in range(OWN):
+        for j in range(owners):
             chosen = jnp.where(here == j, logits[j * children : (j + 1) * children], chosen)
         raised = jnp.exp(chosen * shrink)
         weights = raised / jnp.sum(raised, axis=0, keepdims=True)
         spread.append(
             jnp.concatenate(
-                [jnp.where(here == j, weights, 0.0) for j in range(OWN)], axis=0
+                [jnp.where(here == j, weights, 0.0) for j in range(owners)], axis=0
             ).astype(jnp.bfloat16)
         )
     spread = jnp.concatenate(spread, axis=1)
@@ -483,30 +491,42 @@
 
 
 def dense_sums_kernel(shrink, rows_ref, notes_ref, low_ref, total_ref):
-    sums = weighted_rows(low_ref[...], rows_ref[...], along_lanes(notes_ref[...]), shrink, 256)
-
-    @pl.when(pl.program_id(0) == 0)
+    half = pl.program_id(1)
+    sources, _, tile, width = rows_ref.shape
+    children = low_ref.shape[0] // OWN
+    rows = rows_ref[...].reshape(sources * tile, width)
+    notes = notes_ref[...]
+    lane = lax.broadcasted_iota(jnp.int32, (1, LANES), 1)
+    notes = jnp.where((lax.shift_right_logical(lane, 4) & 1) == half, notes, pltpu.roll(notes, 16, 1))
+    column = lax.broadcasted_iota(jnp.int32, (1, sources * tile), 1)
+    source = lax.broadcasted_iota(jnp.int32, (sources, 1), 0)
+    wide = jnp.concatenate([notes] * (sources * tile // LANES), axis=1)
+    mine = source == lax.shift_right_logical(column, 4)
+    slots = jnp.sum(jnp.where(mine, wide, 0.0), axis=0, keepdims=True).astype(jnp.int32)
+    at = pl.ds(pl.multiple_of(half * children, children), (OWN - 1) * children)
+    sums = weighted_rows(low_ref[at, :], rows, slots - half, shrink, 256, OWN - 1)
+
+    @pl.when((pl.program_id(0) == 0) & (half == 0))
     def _():
-        total_ref[...] = sums
-
-    @pl.when(pl.program_id(0) > 0)
-    def _():
-        total_ref[...] += sums
+        total_ref[...] = jnp.zeros_like(total_ref)
+
+    total_ref[at, :] += sums
 
 
 def dense_sums(arrived, notes, low, shrink):
-    total, width = arrived.shape
-    block = 64 * SHORT
+    sources, short, width = arrived.shape
+    total = sources * short
+    some = 64
     return pl.pallas_call(
         functools.partial(dense_sums_kernel, shrink),
         out_shape=jax.ShapeDtypeStruct(low.shape, jnp.float32),
-        grid=(total // block,),
+        grid=(sources // some, short // TILE),
         in_specs=[
-            pl.BlockSpec((block, width), lambda i: (i, 0)),
-            pl.BlockSpec((block // SHORT, LANES), lambda i: (i, 0)),
-            pl.BlockSpec(low.shape, lambda i: (0, 0), pipeline_mode=pl.Buffered(1)),
+            pl.BlockSpec((some, 1, TILE, width), lambda i, h: (i, h, 0, 0)),
+            pl.BlockSpec((some, LANES), lambda i, h: (i, 0)),
+            pl.BlockSpec(low.shape, lambda i, h: (0, 0), pipeline_mode=pl.Buffered(1)),
         ],
-        out_specs=pl.BlockSpec(low.shape, lambda i: (0, 0)),
+        out_specs=pl.BlockSpec(low.shape, lambda i, h: (0, 0)),
         compiler_params=pltpu.CompilerParams(vmem_limit_bytes=48 << 20),
         cost_estimate=pl.CostEstimate(
             flops=4 * total * width * low.shape[0],
@@ -514,7 +534,7 @@
             transcendentals=total * low.shape[0] // OWN,
         ),
         name="dense_sums",
-    )(arrived, notes, low)
+    )(arrived.reshape(sources, short // TILE, TILE, width), notes, low)
 
 
 def finish_kernel(shrink, per_node, node_ref, total_ref, late_ref, low_ref, unit_ref, out_ref):
@@ -717,7 +737,7 @@
     def short_way():
         arrivals = lax.all_to_all(late, "node", split_axis=0, concat_axis=0, tiled=True)
         flat = low.reshape(OWN * children, width)
-        total = dense_sums(arrived.reshape(devices * SHORT, width), notes, flat, shrink)
+        total = dense_sums(arrived, notes, flat, shrink)
         return finish(
             total, arrivals.reshape(nodes * SHORT, width), flat, unit, here, shrink, nodes
         )

time: 175 us -> 173 us (0.989)
  Pallas kernels: 38.6 us -> 36.8 us
    pallas_call x1, Pallas kernels: 11.9 us -> 10 us  [dense_sums(): pl.pallas_call(functools.partial(dense_sums_kernel, shrink), out_shape=ja...]
  transfers between devices with their start and end apart: 1 -> 1, of which waited for: 0 -> 0; matrix products, arithmetic and copies ran while one was open for 0% -> 0% of each run, Pallas kernels for 7% -> 6%
where the time goes in v5:
time: 173 us
  blocking collectives  131 us (76%)
  Pallas kernels  36.8 us (21%)
  starting transfers between devices  4.13 us (2%)
    all_to_all x1, blocking collectives, body(): lax.all_to_all(packed.reshape(devices, SHORT, width), everyone, split_axi...  109 us
    all_to_all x1, blocking collectives, body(): lax.all_to_all(fresh, 'node', split_axis=0, concat_axis=0, tiled=True)  21.4 us
    pallas_call x1, Pallas kernels, dense_pack(): pl.pallas_call(functools.partial(dense_pack_kernel, outers, owned, nodes)...  14.9 us
    pallas_call x1, Pallas kernels, dense_sums(): pl.pallas_call(functools.partial(dense_sums_kernel, shrink), out_shape=ja...  10 us
    pallas_call x1, Pallas kernels, finish(): pl.pallas_call(functools.partial(finish_kernel, shrink, per_node), out_sh...  4.84 us
    all_to_all x1, starting transfers between devices, short_way(): lax.all_to_all(late, 'node', split_axis=0, concat_axis=0, tiled=True)  4.13 us
    pallas_call x1, Pallas kernels, put_in_order(): pl.pallas_call(functools.partial(order_kernel, per_node), out_shape=(jax....  3.63 us
  transfers between devices with their start and end apart: 1, of which 0 were waited for; matrix products, arithmetic and copies ran while one was open for 0% of the time, Pallas kernels for 6%

profile of v5, /device:TPU:1, one launch (start us, length us, event | category | flops | bytes accessed | tf_op | source)
XLA Modules:
  0.0 173.1 jit_solution(10910908112037521184)
XLA Ops:
  0.6 14.9 %dense_pack.1 = (bf16[4096,1024]{1,0:T(8,128)(2,1)}, bf16[4,128,1024]{2,1,0:T(8,128)(2,1)S(1)}, f32[4,128,1024]{2,1,0:T(8,128)}) custom-call(s32[1]{0:T(128)} %bitcast.7.me_ref, s32[1]{0:T(128)} %bitcast.8.node_ref, s32[1,512]{1,0:T(1,128)} %bitcast.25, s32[24,128]{1,0:T(8,128)} %bitcast.23, bf16[3072,1024]{1,0:T(8,128)(2,1)} %far_rows_ref.1, ...), custom_call_target="tpu_custom_call" | custom-call | tf_op jit(solution)/shard_map/dense_pack/pallas_call | solution.py:356
  15.6 109.3 %all_to_all.19.rows_ref.head_ref = bf16[128,32,1024]{2,1,0:T(8,128)(2,1)} all-to-all(bf16[128,32,1024]{2,1,0:T(8,128)(2,1)} %bitcast.19), channel_id=1, replica_groups=mesh['node'=8,'outer'=16] {'node','outer'}, dimensions={0} | all-to-all | bytes 16777216 | tf_op jit(solution)/shard_map/all_to_all | solution.py:729
  124.9 0.0 copy-start.4
  124.9 0.0 copy-start.5
  124.9 3.4 %collect.1 = (bf16[8,32,1024]{2,1,0:T(8,128)(2,1)}, f32[128,128]{1,0:T(8,128)S(1)}, s32[1]{0:T(128)}) custom-call(s32[1]{0:T(128)} %bitcast.7.me_ref, bf16[128,32,1024]{2,1,0:T(8,128)(2,1)} %all_to_all.19.rows_ref.head_ref, bf16[128,32,1024]{2,1,0:T(8,128)(2,1)} %all_to_all.19.rows_ref.head_ref), custom_call_target="tpu_custom_call" | custom-call | tf_op jit(solution)/shard_map/collect/pallas_call | solution.py:433
  129.0 0.0 copy-done.4
  129.0 0.0 copy-done.5
  129.0 19.0 %conditional.1 = (bf16[8,72,1024]{2,1,0:T(8,128)(2,1)}) conditional(s32[]{:T(128)} %bitcast.12, (bf16[128,32,1024]{2,1,0:T(8,128)(2,1)}, bf16[4,128,1024]{2,1,0:T(8,128)(2,1)S(1)}, f32[128,128]{1,0:T(8,128)S(1)}, bf16[8,32,1024]{2,1,0:T(8,128)(2,1)}, s32[1]{0:T(128)}, /*index=5*/f32[4,128,1024]{2,1,0:T(8,128)}) %tuple.18, (s32[512]{0:T(512)S(1)}, ...), branch_computations={%region_0.0_spmd, %region_1.0_spmd} | conditional | flops 8589934592 | bytes 33570908 | solution.py:753
  129.0 0.0 copy-start.3
  129.0 4.1 %all-to-all-start = ((bf16[8,32,1024]{2,1,0:T(8,128)(2,1)}), bf16[8,32,1024]{2,1,0:T(8,128)(2,1)S(1)}, u32[]{:S(2)}, u32[]{:S(2)}) async-start(bf16[8,32,1024]{2,1,0:T(8,128)(2,1)} %get-tuple-element.31), calls=%async_computation | async-start | bytes 1048576 | tf_op jit(solution)/shard_map/cond/branch_0_fun/all_to_all | solution.py:738
  133.1 0.0 copy-done.3
  133.1 10.0 %dense_sums.1.total_ref = f32[512,1024]{1,0:T(8,128)S(1)} custom-call(bf16[128,2,16,1024]{3,2,1,0:T(8,128)(2,1)} %bitcast.17, f32[128,128]{1,0:T(8,128)S(1)} %get-tuple-element.29.notes_ref, bf16[512,1024]{1,0:T(8,128)(2,1)} %bitcast.21), custom_call_target="tpu_custom_call" | custom-call | flops 8589934592 | bytes 11534336 | tf_op jit(solution)/shard_map/cond/branch_0_fun/dense_sums/pallas_call | solution.py:520
  143.2 0.0 all-to-all-done
  143.2 4.8 %finish.1 = bf16[8,72,1024]{2,1,0:T(8,128)(2,1)} custom-call(s32[1]{0:T(128)} %get-tuple-element.17.node_ref, f32[512,1024]{1,0:T(8,128)S(1)} %dense_sums.1.total_ref, bf16[256,1024]{1,0:T(8,128)(2,1)S(1)} %bitcast.16, bf16[512,1024]{1,0:T(8,128)(2,1)} %bitcast.22, f32[4,128,1024]{2,1,0:T(8,128)} %get-tuple-element.32.unit_ref), custom_call_target="tpu_custom_call" | custom-call | tf_op jit(solution)/shard_map/cond/branch_0_fun/finish/pallas_call | solution.py:570
  148.0 21.4 %all_to_all.20 = bf16[8,72,1024]{2,1,0:T(8,128)(2,1)} all-to-all(bf16[8,72,1024]{2,1,0:T(8,128)(2,1)} %get-tuple-element.91), channel_id=1, replica_groups=mesh['node'=8,'outer'=16] {'node'}, dimensions={0} | all-to-all | bytes 2359296 | tf_op jit(solution)/shard_map/all_to_all | solution.py:754
  169.4 3.6 %put_in_order.1 = (f32[512,1024]{1,0:T(8,128)}, f32[32,1024]{1,0:T(8,128)}) custom-call(bf16[576,1024]{1,0:T(8,128)(2,1)} %bitcast.20), custom_call_target="tpu_custom_call" | custom-call | tf_op jit(solution)/shard_map/put_in_order/pallas_call | solution.py:186
Async XLA Ops:
  124.9 4.1 %copy-start.4 = (s32[3072]{0:T(1024)S(1)}, s32[3072]{0:T(1024)}, u32[]{:S(2)}) copy-start(s32[3072]{0:T(1024)} %param.7) | copy-start | bytes 36868
  124.9 4.1 %copy-start.5 = (s32[512]{0:T(512)S(1)}, s32[512]{0:T(512)}, u32[]{:S(2)}) copy-start(s32[512]{0:T(512)} %param.8) | copy-start | bytes 6148
  129.0 4.1 %copy-start.3 = (bf16[4,128,1024]{2,1,0:T(8,128)(2,1)}, bf16[4,128,1024]{2,1,0:T(8,128)(2,1)S(1)}, u32[]{:S(2)}) copy-start(bf16[4,128,1024]{2,1,0:T(8,128)(2,1)S(1)} %get-tuple-element.30) | copy-start | bytes 3145732 | tf_op jit(solution)/shard_map/cond
  129.0 14.1 %all-to-all-start = ((bf16[8,32,1024]{2,1,0:T(8,128)(2,1)}), bf16[8,32,1024]{2,1,0:T(8,128)(2,1)S(1)}, u32[]{:S(2)}, u32[]{:S(2)}) async-start(bf16[8,32,1024]{2,1,0:T(8,128)(2,1)} %get-tuple-element.31), calls=%async_computation | async-start | bytes 1048576 | tf_op jit(solution)/shard_map/cond/branch_0_fun/all_to_all | solution.py:738

commit v6 on v5

--- a/solution.py
+++ b/solution.py
@@ -508,15 +508,18 @@
 
     @pl.when((pl.program_id(0) == 0) & (half == 0))
     def _():
-        total_ref[...] = jnp.zeros_like(total_ref)
-
-    total_ref[at, :] += sums
+        total_ref[: (OWN - 1) * children, :] = sums
+        total_ref[(OWN - 1) * children :, :] = jnp.zeros((children, width), jnp.float32)
+
+    @pl.when((pl.program_id(0) > 0) | (half > 0))
+    def _():
+        total_ref[at, :] += sums
 
 
 def dense_sums(arrived, notes, low, shrink):
     sources, short, width = arrived.shape
     total = sources * short
-    some = 64
+    some = 128
     return pl.pallas_call(
         functools.partial(dense_sums_kernel, shrink),
         out_shape=jax.ShapeDtypeStruct(low.shape, jnp.float32),

time: 173 us -> 173 us (level)
  blocking collectives: 131 us -> 129 us
where the time goes in v6:
time: 173 us; the launch traced here: 172 us
  blocking collectives  129 us (75%)
  Pallas kernels  37.4 us (22%)
  starting transfers between devices  4.13 us (2%)
    all_to_all x1, blocking collectives, body(): lax.all_to_all(packed.reshape(devices, SHORT, width), everyone, split_axi...  108 us
    all_to_all x1, blocking collectives, body(): lax.all_to_all(fresh, 'node', split_axis=0, concat_axis=0, tiled=True)  21.4 us
    pallas_call x1, Pallas kernels, dense_pack(): pl.pallas_call(functools.partial(dense_pack_kernel, outers, owned, nodes)...  15.8 us
    pallas_call x1, Pallas kernels, dense_sums(): pl.pallas_call(functools.partial(dense_sums_kernel, shrink), out_shape=ja...  9.74 us
    pallas_call x1, Pallas kernels, finish(): pl.pallas_call(functools.partial(finish_kernel, shrink, per_node), out_sh...  4.84 us
    all_to_all x1, starting transfers between devices, short_way(): lax.all_to_all(late, 'node', split_axis=0, concat_axis=0, tiled=True)  4.13 us
    pallas_call x1, Pallas kernels, put_in_order(): pl.pallas_call(functools.partial(order_kernel, per_node), out_shape=(jax....  3.62 us
  transfers between devices with their start and end apart: 1, of which 0 were waited for; matrix products, arithmetic and copies ran while one was open for 0% of the time, Pallas kernels for 6%

profile of v6, /device:TPU:1, one launch (start us, length us, event | category | flops | bytes accessed | tf_op | source)
XLA Modules:
  0.0 172.2 jit_solution(4461127956056172772)
XLA Ops:
  0.6 15.8 %dense_pack.1 = (bf16[4096,1024]{1,0:T(8,128)(2,1)}, bf16[4,128,1024]{2,1,0:T(8,128)(2,1)S(1)}, f32[4,128,1024]{2,1,0:T(8,128)}) custom-call(s32[1]{0:T(128)} %bitcast.7.me_ref, s32[1]{0:T(128)} %bitcast.8.node_ref, s32[1,512]{1,0:T(1,128)} %bitcast.25, s32[24,128]{1,0:T(8,128)} %bitcast.23, bf16[3072,1024]{1,0:T(8,128)(2,1)} %far_rows_ref.1, ...), custom_call_target="tpu_custom_call" | custom-call | tf_op jit(solution)/shard_map/dense_pack/pallas_call | solution.py:356
  16.4 107.9 %all_to_all.19.rows_ref.head_ref = bf16[128,32,1024]{2,1,0:T(8,128)(2,1)} all-to-all(bf16[128,32,1024]{2,1,0:T(8,128)(2,1)} %bitcast.19), channel_id=1, replica_groups=mesh['node'=8,'outer'=16] {'node','outer'}, dimensions={0} | all-to-all | bytes 16777216 | tf_op jit(solution)/shard_map/all_to_all | solution.py:732
  124.3 0.0 copy-start.4
  124.3 0.0 copy-start.5
  124.3 3.4 %collect.1 = (bf16[8,32,1024]{2,1,0:T(8,128)(2,1)}, f32[128,128]{1,0:T(8,128)S(1)}, s32[1]{0:T(128)}) custom-call(s32[1]{0:T(128)} %bitcast.7.me_ref, bf16[128,32,1024]{2,1,0:T(8,128)(2,1)} %all_to_all.19.rows_ref.head_ref, bf16[128,32,1024]{2,1,0:T(8,128)(2,1)} %all_to_all.19.rows_ref.head_ref), custom_call_target="tpu_custom_call" | custom-call | tf_op jit(solution)/shard_map/collect/pallas_call | solution.py:433
  128.4 0.0 copy-done.4
  128.4 0.0 copy-done.5
  128.4 18.8 %conditional.1 = (bf16[8,72,1024]{2,1,0:T(8,128)(2,1)}) conditional(s32[]{:T(128)} %bitcast.12, (bf16[128,32,1024]{2,1,0:T(8,128)(2,1)}, bf16[4,128,1024]{2,1,0:T(8,128)(2,1)S(1)}, f32[128,128]{1,0:T(8,128)S(1)}, bf16[8,32,1024]{2,1,0:T(8,128)(2,1)}, s32[1]{0:T(128)}, /*index=5*/f32[4,128,1024]{2,1,0:T(8,128)}) %tuple.18, (s32[512]{0:T(512)S(1)}, ...), branch_computations={%region_0.0_spmd, %region_1.0_spmd} | conditional | flops 8589934592 | bytes 33570908 | solution.py:756
  128.4 0.0 copy-start.3
  128.4 4.1 %all-to-all-start = ((bf16[8,32,1024]{2,1,0:T(8,128)(2,1)}), bf16[8,32,1024]{2,1,0:T(8,128)(2,1)S(1)}, u32[]{:S(2)}, u32[]{:S(2)}) async-start(bf16[8,32,1024]{2,1,0:T(8,128)(2,1)} %get-tuple-element.31), calls=%async_computation | async-start | bytes 1048576 | tf_op jit(solution)/shard_map/cond/branch_0_fun/all_to_all | solution.py:741
  132.6 0.0 copy-done.3
  132.6 9.7 %dense_sums.1.total_ref = f32[512,1024]{1,0:T(8,128)S(1)} custom-call(bf16[128,2,16,1024]{3,2,1,0:T(8,128)(2,1)} %bitcast.17, f32[128,128]{1,0:T(8,128)S(1)} %get-tuple-element.29.notes_ref, bf16[512,1024]{1,0:T(8,128)(2,1)} %bitcast.21), custom_call_target="tpu_custom_call" | custom-call | flops 8589934592 | bytes 11534336 | tf_op jit(solution)/shard_map/cond/branch_0_fun/dense_sums/pallas_call | solution.py:523
  142.3 0.0 all-to-all-done
  142.3 4.8 %finish.1 = bf16[8,72,1024]{2,1,0:T(8,128)(2,1)} custom-call(s32[1]{0:T(128)} %get-tuple-element.17.node_ref, f32[512,1024]{1,0:T(8,128)S(1)} %dense_sums.1.total_ref, bf16[256,1024]{1,0:T(8,128)(2,1)S(1)} %bitcast.16, bf16[512,1024]{1,0:T(8,128)(2,1)} %bitcast.22, f32[4,128,1024]{2,1,0:T(8,128)} %get-tuple-element.32.unit_ref), custom_call_target="tpu_custom_call" | custom-call | tf_op jit(solution)/shard_map/cond/branch_0_fun/finish/pallas_call | solution.py:573
  147.2 21.4 %all_to_all.20 = bf16[8,72,1024]{2,1,0:T(8,128)(2,1)} all-to-all(bf16[8,72,1024]{2,1,0:T(8,128)(2,1)} %get-tuple-element.91), channel_id=1, replica_groups=mesh['node'=8,'outer'=16] {'node'}, dimensions={0} | all-to-all | bytes 2359296 | tf_op jit(solution)/shard_map/all_to_all | solution.py:757
  168.6 3.6 %put_in_order.1 = (f32[512,1024]{1,0:T(8,128)}, f32[32,1024]{1,0:T(8,128)}) custom-call(bf16[576,1024]{1,0:T(8,128)(2,1)} %bitcast.20), custom_call_target="tpu_custom_call" | custom-call | tf_op jit(solution)/shard_map/put_in_order/pallas_call | solution.py:186
Async XLA Ops:
  124.3 4.1 %copy-start.4 = (s32[3072]{0:T(1024)S(1)}, s32[3072]{0:T(1024)}, u32[]{:S(2)}) copy-start(s32[3072]{0:T(1024)} %param.7) | copy-start | bytes 36868
  124.3 4.1 %copy-start.5 = (s32[512]{0:T(512)S(1)}, s32[512]{0:T(512)}, u32[]{:S(2)}) copy-start(s32[512]{0:T(512)} %param.8) | copy-start | bytes 6148
  128.4 4.1 %copy-start.3 = (bf16[4,128,1024]{2,1,0:T(8,128)(2,1)}, bf16[4,128,1024]{2,1,0:T(8,128)(2,1)S(1)}, u32[]{:S(2)}) copy-start(bf16[4,128,1024]{2,1,0:T(8,128)(2,1)S(1)} %get-tuple-element.30) | copy-start | bytes 3145732 | tf_op jit(solution)/shard_map/cond
  128.4 13.9 %all-to-all-start = ((bf16[8,32,1024]{2,1,0:T(8,128)(2,1)}), bf16[8,32,1024]{2,1,0:T(8,128)(2,1)S(1)}, u32[]{:S(2)}, u32[]{:S(2)}) async-start(bf16[8,32,1024]{2,1,0:T(8,128)(2,1)} %get-tuple-element.31), calls=%async_computation | async-start | bytes 1048576 | tf_op jit(solution)/shard_map/cond/branch_0_fun/all_to_all | solution.py:741
